TPU v7x, 512 devices: a whole 4x8x8 slice. The times are simulated.
512 devices in a mesh: pole: 16 (over z_lo, x), dom: 32 (over y, z_hi, core).
Axes of the slice: x: 4, y: 8, z: 8 (z_hi: 2, z_lo: 4; z = z_hi * 4 + z_lo), core: 2. Of those that a mesh axis runs over, the one named last changes fastest.
Arguments:
- y_interior: float32 [32, 512, 256], P('dom', 'pole'), may hold values from -6 to 6
- y_separator: float32 [32, 64, 256], P('dom'), may hold values from -6 to 6
- green: float32 [2, 16, 32, 512, 512], P(None, 'pole', 'dom'), as said below
- pole_data: float32 [4, 16], P(None, 'pole'), as said below
- coupling: float32 [32, 2, 64, 128], P('dom')
- sep_block: float32 [32, 64, 64], P('dom'), as said below
- iface_rows: int32 [32, 2, 128], P('dom'), may hold values from 0 to 511, as said below
Outputs:
- filtered: float32 [32, 512, 256], P('dom', 'pole')
- filtered_sep: float32 [32, 64, 256], P('dom', 'pole')
Inputs may be any that keep to these rules, and one draw needn't show every extreme that they name: green[:, p, d] holds the real and imaginary parts of the inverse of z[p] I - H[d], where H[d] is a real symmetric matrix of order 512 and z[p] is the pole of pole_data. `pole_data`: every pole lies in the upper half plane with imaginary part 0.3 or more. `sep_block`: each block is symmetric. iface_rows[d, 0] and iface_rows[d, 1] each list 128 distinct rows of domain d, and no row is in both.
All inputs are finite; a program needn't handle non-finite values.
Results may differ from a plain program's by a relative error of at most 0.00095.
Values sent between devices are 32-bit elements; how exact they have to be, the bound alone decides.
No kernel may reach another device: no remote copies, remote signals or barrier semaphores. Data moves between devices by JAX's collectives and lax.ppermute only.
A program may use at most 64 MiB of HBM per device.

v0:
```python
import jax
import jax.numpy as jnp
from jax import lax
from jax.sharding import PartitionSpec as P

precise_mode = lax.Precision.HIGHEST


def from_behind(value, axis, steps):
    count = lax.axis_size(axis)
    first, last = (max(0, -steps), min(count, count - steps))
    return lax.ppermute(value, axis, [(source, source + steps) for source in range(first, last)])


def matmul(left_side, right_side):
    return jnp.matmul(left_side, right_side, precision=precise_mode)


def complex_mul(left_factor, right_factor):
    return jnp.stack(
        [
            matmul(left_factor[0], right_factor[0]) - matmul(left_factor[1], right_factor[1]),
            matmul(left_factor[0], right_factor[1]) + matmul(left_factor[1], right_factor[0]),
        ]
    )


def real_left(real_mat, right_factor):
    return jnp.stack([matmul(real_mat, right_factor[0]), matmul(real_mat, right_factor[1])])


def real_right(left_factor, real_mat):
    return jnp.stack([matmul(left_factor[0], real_mat), matmul(left_factor[1], real_mat)])


def complex_solve(pivot_blk, right_hand):
    sep_order = pivot_blk.shape[-1]
    upper_half = jnp.concatenate([pivot_blk[0], -pivot_blk[1]], axis=1)
    lower_half = jnp.concatenate([pivot_blk[1], pivot_blk[0]], axis=1)
    system = jnp.concatenate([upper_half, lower_half], axis=0)
    stacked = jnp.concatenate([right_hand[0], right_hand[1]], axis=0)
    normal_matrix = matmul(system.T, system)
    factor = jnp.linalg.cholesky(normal_matrix)
    solved = jax.scipy.linalg.cho_solve((factor, True), matmul(system.T, stacked))
    return jnp.stack([solved[:sep_order], solved[sep_order:]])


def domain_pieces(green_dom, interior_v, coupling_dom, rows_dom):
    right_rows = rows_dom[0]
    left_rows = rows_dom[1]
    right_map = coupling_dom[0]
    left_map = coupling_dom[1]
    inner_u = real_right(jnp.take(green_dom, right_rows, axis=2), right_map.T)
    inner_w = real_right(jnp.take(green_dom, left_rows, axis=2), left_map.T)
    own_pivot = real_left(right_map, jnp.take(inner_u, right_rows, axis=1))
    own_lower = -real_left(right_map, jnp.take(inner_w, right_rows, axis=1))
    own_right = real_left(right_map, jnp.take(interior_v, right_rows, axis=1))
    next_pack = jnp.concatenate(
        [
            real_left(left_map, jnp.take(inner_w, left_rows, axis=1)),
            real_left(left_map, jnp.take(inner_u, left_rows, axis=1)),
            real_left(left_map, jnp.take(interior_v, left_rows, axis=1)),
        ],
        axis=-1,
    )
    return (inner_u, inner_w, own_pivot, own_lower, own_right, next_pack)


def shards(y_interior, y_separator, green, pole_data, coupling, sep_block, iface_rows):
    green_local = green[:, 0]
    local_count = green_local.shape[1]
    sep_order = sep_block.shape[-1]
    interior_v = jnp.einsum(
        "cdij,djm->dcim",
        green_local,
        lax.all_gather(y_interior, "pole", axis=1, tiled=True),
        precision=precise_mode,
    )
    pieces = [domain_pieces(green_local[:, 0], interior_v[0], coupling[0], iface_rows[0])]
    inner_u = jnp.stack([piece[0] for piece in pieces])
    inner_w = jnp.stack([piece[1] for piece in pieces])
    own_pivot = jnp.stack([piece[2] for piece in pieces])
    own_lower = jnp.stack([piece[3] for piece in pieces])
    own_right = jnp.stack([piece[4] for piece in pieces])
    incoming = from_behind(pieces[0][5], "dom", -1)
    shifted = jnp.stack([piece[5] for piece in pieces[1:]] + [incoming])
    column = pole_data[:, 0]
    identity = jnp.eye(sep_order, dtype=jnp.float32)
    domain_pos = lax.axis_index("dom")
    global_pos = domain_pos * local_count + jnp.arange(local_count, dtype=jnp.int32)
    not_first = (global_pos > 0).astype(jnp.float32)[:, None, None, None]
    shift_eye = jnp.stack([column[0] * identity, column[1] * identity])
    separator_own = jnp.stack([sep_block, jnp.zeros_like(sep_block)], axis=1)
    pivot_blk = shift_eye[None] - separator_own - own_pivot - shifted[..., :sep_order]
    upper_blk = -shifted[..., sep_order : 2 * sep_order]
    right_blk = (
        jnp.stack([y_separator, jnp.zeros_like(y_separator)], axis=1)
        + own_right
        + shifted[..., 2 * sep_order :]
    )
    lower_blk = own_lower * not_first
    solve_many = jax.vmap(complex_solve)
    mul_many = jax.vmap(complex_mul)
    levels = (lax.axis_size("dom") * local_count).bit_length() - 1
    for level_index in range(levels):
        stride = 1 << level_index
        hops = max(stride // local_count, 1)
        scaled = solve_many(pivot_blk, jnp.concatenate([lower_blk, upper_blk, right_blk], axis=-1))
        below_dev = from_behind(scaled, "dom", hops)
        above_dev = from_behind(scaled, "dom", -hops)
        left_terms = mul_many(lower_blk, below_dev)
        right_terms = mul_many(upper_blk, above_dev)
        lower_blk = -left_terms[..., :sep_order]
        upper_blk = -right_terms[..., sep_order : 2 * sep_order]
        pivot_blk = (
            pivot_blk - left_terms[..., sep_order : 2 * sep_order] - right_terms[..., :sep_order]
        )
        right_blk = right_blk - left_terms[..., 2 * sep_order :] - right_terms[..., 2 * sep_order :]
    solution = solve_many(pivot_blk, right_blk)
    last_before = from_behind(solution, "dom", 1)
    previous = jnp.concatenate([last_before, solution[:-1]], axis=0)
    field_value = interior_v + mul_many(inner_u, solution) + mul_many(inner_w, previous)
    weighted = column[2] * field_value[:, 0] - column[3] * field_value[:, 1]
    weighted_sep = column[2] * solution[:, 0] - column[3] * solution[:, 1]
    out_interior, out_separator = (
        lax.psum_scatter(weighted, "pole", scatter_dimension=1, tiled=True),
        lax.psum_scatter(weighted_sep, "pole", scatter_dimension=1, tiled=True),
    )
    return (out_interior, out_separator)


def solution(mesh):
    return jax.shard_map(
        shards,
        mesh=mesh,
        in_specs=(
            P("dom", "pole", None),
            P("dom", None, None),
            P(None, "pole", "dom", None, None),
            P(None, "pole"),
            P("dom", None, None, None),
            P("dom", None, None),
            P("dom", None, None),
        ),
        out_specs=(P("dom", "pole", None), P("dom", "pole", None)),
        check_vma=False,
    )
```

profile of v0, /device:TPU:16, one launch (start us, length us, event | category | flops | bytes accessed | tf_op | source)
XLA Modules:
  0.0 583.5 jit_solution(37094456884448511)
XLA Ops:
  7.2 2.9 copy.41
  10.1 47.9 %all_gather.3 = f32[1,512,256]{2,1,0:T(8,128)S(1)} all-gather(f32[1,32,256]{2,1,0:T(8,128)S(1)} %copy-done.5), channel_id=1, replica_groups=mesh['pole'=16,'dom'=32] {'pole'}, dimensions={1}, use_global_device_ids=true | all-gather | bytes 557056 | tf_op jit(solution)/shard_map/all_gather | solution.py:76
  58.0 3.5 fusion
  79.7 2.2 collective-permute-start
  88.0 11.7 %custom-call.25 = f32[1,128,128]{2,1,0:T(8,128)S(1)} custom-call(f32[1,128,128]{2,1,0:T(8,128)S(1)} %fusion.105), custom_call_target="Cholesky" | custom-call | tf_op jit(solution)/shard_map/vmap(jit(cholesky))/cholesky | solution.py:43
  101.1 9.8 %custom-call.26 = f32[1,1,128,128]{2,3,1,0:T(8,128)S(1)} custom-call(f32[1,1,128,128]{3,2,1,0:T(8,128)S(1)} %fusion.91), custom_call_target="InvertDiagBlocksLowerTriangular" | custom-call | tf_op jit(solution)/shard_map/vmap(jit(_cho_solve))/triangular_solve | solution.py:44
  112.1 8.2 %collective-permute-start.2 = (f32[1,2,64,384]{3,2,1,0:T(8,128)S(1)}, f32[1,2,64,384]{3,2,1,0:T(8,128)S(1)}, u32[]{:S(2)}, u32[]{:S(2)}) collective-permute-start(f32[1,2,64,384]{3,2,1,0:T(8,128)S(1)} %maximum_bitcast_fusion.4), channel_id=1, source_target_pairs={{1,0},{2,1},{3,2},{4,3},{5,4},{6,5},{7,6},{8,7},{9,8},{10,9},{11,1... | collective-permute-start | bytes 589832 | tf_op jit(solution)/shard_map/ppermute | solution.py:12
  120.3 2.4 collective-permute-start.1
  124.4 7.7 %collective-permute-done.1 = f32[1,2,64,384]{3,2,1,0:T(8,128)S(1)} collective-permute-done((f32[1,2,64,384]{3,2,1,0:T(8,128)S(1)}, f32[1,2,64,384]{3,2,1,0:T(8,128)S(1)}, u32[]{:S(2)}, u32[]{:S(2)}) %collective-permute-start.1) | collective-permute-done | bytes 196640 | tf_op jit(solution)/shard_map/ppermute | solution.py:12
  133.8 11.7 %custom-call.27 = f32[1,128,128]{2,1,0:T(8,128)S(1)} custom-call(f32[1,128,128]{2,1,0:T(8,128)S(1)} %fusion.104), custom_call_target="Cholesky" | custom-call | tf_op jit(solution)/shard_map/vmap(jit(cholesky))/cholesky | solution.py:43
  146.8 9.8 %custom-call.28 = f32[1,1,128,128]{2,3,1,0:T(8,128)S(1)} custom-call(f32[1,1,128,128]{3,2,1,0:T(8,128)S(1)} %fusion.92), custom_call_target="InvertDiagBlocksLowerTriangular" | custom-call | tf_op jit(solution)/shard_map/vmap(jit(_cho_solve))/triangular_solve | solution.py:44
  157.8 4.4 collective-permute-start.4
  162.3 5.5 collective-permute-start.3
  167.8 4.3 collective-permute-done.4
  176.3 11.7 %custom-call.29 = f32[1,128,128]{2,1,0:T(8,128)S(1)} custom-call(f32[1,128,128]{2,1,0:T(8,128)S(1)} %fusion.103), custom_call_target="Cholesky" | custom-call | tf_op jit(solution)/shard_map/vmap(jit(cholesky))/cholesky | solution.py:43
  189.4 9.8 %custom-call.30 = f32[1,1,128,128]{2,3,1,0:T(8,128)S(1)} custom-call(f32[1,1,128,128]{3,2,1,0:T(8,128)S(1)} %fusion.93), custom_call_target="InvertDiagBlocksLowerTriangular" | custom-call | tf_op jit(solution)/shard_map/vmap(jit(_cho_solve))/triangular_solve | solution.py:44
  200.4 2.4 collective-permute-start.6
  202.7 5.1 collective-permute-start.5
  207.8 2.9 collective-permute-done.6
  213.6 11.7 %custom-call.31 = f32[1,128,128]{2,1,0:T(8,128)S(1)} custom-call(f32[1,128,128]{2,1,0:T(8,128)S(1)} %fusion.102), custom_call_target="Cholesky" | custom-call | tf_op jit(solution)/shard_map/vmap(jit(cholesky))/cholesky | solution.py:43
  226.7 9.8 %custom-call.32 = f32[1,1,128,128]{2,3,1,0:T(8,128)S(1)} custom-call(f32[1,1,128,128]{3,2,1,0:T(8,128)S(1)} %fusion.94), custom_call_target="InvertDiagBlocksLowerTriangular" | custom-call | tf_op jit(solution)/shard_map/vmap(jit(_cho_solve))/triangular_solve | solution.py:44
  239.6 8.2 %collective-permute-start.7 = (f32[1,2,64,384]{3,2,1,0:T(8,128)S(1)}, f32[1,2,64,384]{3,2,1,0:T(8,128)S(1)}, u32[]{:S(2)}, u32[]{:S(2)}) collective-permute-start(f32[1,2,64,384]{3,2,1,0:T(8,128)S(1)} %maximum_bitcast_fusion.19), channel_id=1, source_target_pairs={{0,8},{1,9},{2,10},{3,11},{4,12},{5,13},{6,14},{7,15},{8,16},{9,17... | collective-permute-start | bytes 589832 | tf_op jit(solution)/shard_map/ppermute | solution.py:12
  247.8 5.8 collective-permute-done.8
  256.6 11.7 %custom-call.33 = f32[1,128,128]{2,1,0:T(8,128)S(1)} custom-call(f32[1,128,128]{2,1,0:T(8,128)S(1)} %fusion.101), custom_call_target="Cholesky" | custom-call | tf_op jit(solution)/shard_map/vmap(jit(cholesky))/cholesky | solution.py:43
  269.6 9.8 %custom-call.34 = f32[1,1,128,128]{2,3,1,0:T(8,128)S(1)} custom-call(f32[1,1,128,128]{3,2,1,0:T(8,128)S(1)} %fusion.95), custom_call_target="InvertDiagBlocksLowerTriangular" | custom-call | tf_op jit(solution)/shard_map/vmap(jit(_cho_solve))/triangular_solve | solution.py:44
  281.9 8.9 %collective-permute-start.9 = (f32[1,2,64,384]{3,2,1,0:T(8,128)S(1)}, f32[1,2,64,384]{3,2,1,0:T(8,128)S(1)}, u32[]{:S(2)}, u32[]{:S(2)}) collective-permute-start(f32[1,2,64,384]{3,2,1,0:T(8,128)S(1)} %maximum_bitcast_fusion.24), channel_id=1, source_target_pairs={{0,16},{1,17},{2,18},{3,19},{4,20},{5,21},{6,22},{7,23},{8,24},{9,... | collective-permute-start | bytes 589832 | tf_op jit(solution)/shard_map/ppermute | solution.py:12
  290.9 5.9 %collective-permute-done.10 = f32[1,2,64,384]{3,2,1,0:T(8,128)S(1)} collective-permute-done((f32[1,2,64,384]{3,2,1,0:T(8,128)S(1)}, f32[1,2,64,384]{3,2,1,0:T(8,128)S(1)}, u32[]{:S(2)}, u32[]{:S(2)}) %collective-permute-start.10) | collective-permute-done | bytes 196640 | tf_op jit(solution)/shard_map/ppermute | solution.py:12
  299.3 11.7 %custom-call.35 = f32[1,128,128]{2,1,0:T(8,128)S(1)} custom-call(f32[1,128,128]{2,1,0:T(8,128)S(1)} %fusion.100), custom_call_target="Cholesky" | custom-call | tf_op jit(solution)/shard_map/vmap(jit(cholesky))/cholesky | solution.py:43
  312.4 9.8 %custom-call.15 = f32[1,1,128,128]{2,3,1,0:T(8,128)S(1)} custom-call(f32[1,1,128,128]{3,2,1,0:T(8,128)S(1)} %fusion.96), custom_call_target="InvertDiagBlocksLowerTriangular" | custom-call | tf_op jit(solution)/shard_map/vmap(jit(_cho_solve))/triangular_solve | solution.py:44
  330.6 5.0 collective-permute-done.11
  342.3 143.4 %all-reduce.5.cloned.1.call-done = f32[1,64,256]{2,1,0:T(8,128)} async-done(((f32[1,64,256]{2,1,0:T(8,128)}), f32[1,64,256]{2,1,0:T(8,128)}) %all-reduce.5.cloned.1.call-update) | async-done | bytes 65552
  487.1 89.4 %reduce-scatter.3.cloned.1.call-done = f32[1,32,256]{2,1,0:T(8,128)} async-done(((f32[1,512,256]{2,1,0:T(8,128)}), f32[1,32,256]{2,1,0:T(8,128)}) %reduce-scatter.3.cloned.1.call-update) | async-done | bytes 32784 | tf_op jit(solution)/shard_map/reduce_scatter | solution.py:126
  (245 shorter events, 71.6 us)
Async XLA Ops:
  7.2 2.9 copy-start.5
  7.2 50.8 %copy-start.9 = (s32[1,2,128]{2,1,0:T(2,128)S(1)}, s32[1,2,128]{2,1,0:T(2,128)}, u32[]{:S(2)}) copy-start(s32[1,2,128]{2,1,0:T(2,128)} %param.22) | copy-start | bytes 3076
  7.2 478.6 %all-reduce.5.cloned.1.call-start = ((), (), s32[]{:S(2)}) async-start(), calls=%async_computation.2 | async-start | bytes 131072
  58.0 12.7 %copy-start.8 = (pred[128]{0:T(512)(128)(4,1)}, pred[128]{0:T(512)(128)(4,1)S(1)}, u32[]{:S(2)}) copy-start(pred[128]{0:T(512)(128)(4,1)S(1)} %get-tuple-element.4) | copy-start | bytes 388
  65.3 2.6 copy-start.1
  66.1 4.0 copy-start
  75.0 8.3 %copy-start.3 = (f32[2,128,256]{2,0,1:T(2,128)S(1)}, f32[2,128,256]{2,0,1:T(2,128)}, u32[]{:S(2)}) copy-start(f32[2,128,256]{2,0,1:T(2,128)} %get-tuple-element.93) | copy-start | bytes 786436
  75.1 8.7 %copy-start.7 = (f32[4,1]{0,1:T(1,128)S(1)}, f32[4,1]{0,1:T(1,128)}, u32[]{:S(2)}) copy-start(f32[4,1]{0,1:T(1,128)} %param.19) | copy-start | bytes 52
  77.5 9.8 %copy-start.6 = (f32[1,64,64]{2,1,0:T(8,128)S(1)}, f32[1,64,64]{2,1,0:T(8,128)}, u32[]{:S(2)}) copy-start(f32[1,64,64]{2,1,0:T(8,128)} %param.21) | copy-start | bytes 49156
  78.0 9.4 %copy-start.4 = (f32[1,64,256]{2,1,0:T(8,128)S(1)}, f32[1,64,256]{2,1,0:T(8,128)}, u32[]{:S(2)}) copy-start(f32[1,64,256]{2,1,0:T(8,128)} %param.17) | copy-start | bytes 196612
  79.7 7.6 %collective-permute-start = (f32[2,64,384]{2,1,0:T(8,128)}, f32[2,64,384]{2,1,0:T(8,128)S(1)}, u32[]{:S(2)}, u32[]{:S(2)}) collective-permute-start(f32[2,64,384]{2,1,0:T(8,128)} %maximum_maximum_fusion), channel_id=1, source_target_pairs={{1,0},{2,1},{3,2},{4,3},{5,4},{6,5},{7,6},{8,7},{9,8},{10,9},{11,1... | collective-permute-start | bytes 589832 | tf_op jit(solution)/shard_map/ppermute | solution.py:12
  112.1 11.4 %collective-permute-start.2 = (f32[1,2,64,384]{3,2,1,0:T(8,128)S(1)}, f32[1,2,64,384]{3,2,1,0:T(8,128)S(1)}, u32[]{:S(2)}, u32[]{:S(2)}) collective-permute-start(f32[1,2,64,384]{3,2,1,0:T(8,128)S(1)} %maximum_bitcast_fusion.4), channel_id=1, source_target_pairs={{1,0},{2,1},{3,2},{4,3},{5,4},{6,5},{7,6},{8,7},{9,8},{10,9},{11,1... | collective-permute-start | bytes 589832 | tf_op jit(solution)/shard_map/ppermute | solution.py:12
  120.3 11.8 %collective-permute-start.1 = (f32[1,2,64,384]{3,2,1,0:T(8,128)S(1)}, f32[1,2,64,384]{3,2,1,0:T(8,128)S(1)}, u32[]{:S(2)}, u32[]{:S(2)}) collective-permute-start(f32[1,2,64,384]{3,2,1,0:T(8,128)S(1)} %maximum_bitcast_fusion.4), channel_id=1, source_target_pairs={{0,1},{1,2},{2,3},{3,4},{4,5},{5,6},{6,7},{7,8},{8,9},{9,10},{10,1... | collective-permute-start | bytes 589832 | tf_op jit(solution)/shard_map/ppermute | solution.py:12
  157.8 14.3 %collective-permute-start.4 = (f32[1,2,64,384]{3,2,1,0:T(8,128)S(1)}, f32[1,2,64,384]{3,2,1,0:T(8,128)S(1)}, u32[]{:S(2)}, u32[]{:S(2)}) collective-permute-start(f32[1,2,64,384]{3,2,1,0:T(8,128)S(1)} %maximum_bitcast_fusion.9), channel_id=1, source_target_pairs={{2,0},{3,1},{4,2},{5,3},{6,4},{7,5},{8,6},{9,7},{10,8},{11,9},{12,... | collective-permute-start | bytes 589832 | tf_op jit(solution)/shard_map/ppermute | solution.py:12
  162.3 12.4 %collective-permute-start.3 = (f32[1,2,64,384]{3,2,1,0:T(8,128)S(1)}, f32[1,2,64,384]{3,2,1,0:T(8,128)S(1)}, u32[]{:S(2)}, u32[]{:S(2)}) collective-permute-start(f32[1,2,64,384]{3,2,1,0:T(8,128)S(1)} %maximum_bitcast_fusion.9), channel_id=1, source_target_pairs={{0,2},{1,3},{2,4},{3,5},{4,6},{5,7},{6,8},{7,9},{8,10},{9,11},{10,... | collective-permute-start | bytes 589832 | tf_op jit(solution)/shard_map/ppermute | solution.py:12
  200.4 10.4 %collective-permute-start.6 = (f32[1,2,64,384]{3,2,1,0:T(8,128)S(1)}, f32[1,2,64,384]{3,2,1,0:T(8,128)S(1)}, u32[]{:S(2)}, u32[]{:S(2)}) collective-permute-start(f32[1,2,64,384]{3,2,1,0:T(8,128)S(1)} %maximum_bitcast_fusion.14), channel_id=1, source_target_pairs={{4,0},{5,1},{6,2},{7,3},{8,4},{9,5},{10,6},{11,7},{12,8},{13,9},{1... | collective-permute-start | bytes 589832 | tf_op jit(solution)/shard_map/ppermute | solution.py:12
  202.7 9.2 %collective-permute-start.5 = (f32[1,2,64,384]{3,2,1,0:T(8,128)S(1)}, f32[1,2,64,384]{3,2,1,0:T(8,128)S(1)}, u32[]{:S(2)}, u32[]{:S(2)}) collective-permute-start(f32[1,2,64,384]{3,2,1,0:T(8,128)S(1)} %maximum_bitcast_fusion.14), channel_id=1, source_target_pairs={{0,4},{1,5},{2,6},{3,7},{4,8},{5,9},{6,10},{7,11},{8,12},{9,13},{1... | collective-permute-start | bytes 589832 | tf_op jit(solution)/shard_map/ppermute | solution.py:12
  237.7 16.0 %collective-permute-start.8 = (f32[1,2,64,384]{3,2,1,0:T(8,128)S(1)}, f32[1,2,64,384]{3,2,1,0:T(8,128)S(1)}, u32[]{:S(2)}, u32[]{:S(2)}) collective-permute-start(f32[1,2,64,384]{3,2,1,0:T(8,128)S(1)} %maximum_bitcast_fusion.19), channel_id=1, source_target_pairs={{8,0},{9,1},{10,2},{11,3},{12,4},{13,5},{14,6},{15,7},{16,8},{17,9... | collective-permute-start | bytes 589832 | tf_op jit(solution)/shard_map/ppermute | solution.py:12
  239.6 15.3 %collective-permute-start.7 = (f32[1,2,64,384]{3,2,1,0:T(8,128)S(1)}, f32[1,2,64,384]{3,2,1,0:T(8,128)S(1)}, u32[]{:S(2)}, u32[]{:S(2)}) collective-permute-start(f32[1,2,64,384]{3,2,1,0:T(8,128)S(1)} %maximum_bitcast_fusion.19), channel_id=1, source_target_pairs={{0,8},{1,9},{2,10},{3,11},{4,12},{5,13},{6,14},{7,15},{8,16},{9,17... | collective-permute-start | bytes 589832 | tf_op jit(solution)/shard_map/ppermute | solution.py:12
  280.6 16.2 %collective-permute-start.10 = (f32[1,2,64,384]{3,2,1,0:T(8,128)S(1)}, f32[1,2,64,384]{3,2,1,0:T(8,128)S(1)}, u32[]{:S(2)}, u32[]{:S(2)}) collective-permute-start(f32[1,2,64,384]{3,2,1,0:T(8,128)S(1)} %maximum_bitcast_fusion.24), channel_id=1, source_target_pairs={{16,0},{17,1},{18,2},{19,3},{20,4},{21,5},{22,6},{23,7},{24,8},{25... | collective-permute-start | bytes 589832 | tf_op jit(solution)/shard_map/ppermute | solution.py:12
  281.9 15.8 %collective-permute-start.9 = (f32[1,2,64,384]{3,2,1,0:T(8,128)S(1)}, f32[1,2,64,384]{3,2,1,0:T(8,128)S(1)}, u32[]{:S(2)}, u32[]{:S(2)}) collective-permute-start(f32[1,2,64,384]{3,2,1,0:T(8,128)S(1)} %maximum_bitcast_fusion.24), channel_id=1, source_target_pairs={{0,16},{1,17},{2,18},{3,19},{4,20},{5,21},{6,22},{7,23},{8,24},{9,... | collective-permute-start | bytes 589832 | tf_op jit(solution)/shard_map/ppermute | solution.py:12
  324.4 11.1 %collective-permute-start.11 = (f32[1,2,64,256]{3,2,1,0:T(8,128)S(1)}, f32[1,2,64,256]{3,2,1,0:T(8,128)S(1)}, u32[]{:S(2)}, u32[]{:S(2)}) collective-permute-start(f32[1,2,64,256]{3,2,1,0:T(8,128)S(1)} %maximum_bitcast_fusion.30), channel_id=1, source_target_pairs={{0,1},{1,2},{2,3},{3,4},{4,5},{5,6},{6,7},{7,8},{8,9},{9,10},{10,1... | collective-permute-start | bytes 393224 | tf_op jit(solution)/shard_map/ppermute | solution.py:12
  329.7 246.7 %reduce-scatter.3.cloned.1.call-start = ((), (), s32[]{:S(2)}) async-start(), calls=%async_computation.1 | async-start | bytes 557056 | tf_op jit(solution)/shard_map/reduce_scatter | solution.py:126
  330.6 7.5 %copy-start.2 = (f32[1,1,512,256]{3,2,0,1:T(8,128)S(1)}, f32[1,1,512,256]{3,2,0,1:T(8,128)}, u32[]{:S(2)}) copy-start(f32[1,1,512,256]{3,2,0,1:T(8,128)} %fusion.4) | copy-start | bytes 1572868
Sparse Core Ops, SparseCore 0:
  329.8 155.8 all-reduce.4
  489.1 87.2 reduce-scatter.2
where the time goes:
time: 592 us; the launch traced here: 583 us
  waiting for transfers between devices  267 us (45%)
  other arithmetic  150 us (25%)
  starting transfers between devices  52.8 us (9%)
  blocking collectives  47.9 us (8%)
  matrix products  30.6 us (5%)
  local copies, waits for them, and re-layouts  18.3 us (3%)
  between operations  16.6 us (3%)
    unnamed x3, waiting for transfers between devices  143 us
    reduce_scatter x1, waiting for transfers between devices, shards(): lax.psum_scatter(weighted, 'pole', scatter_dimension=1, tiled=True)  89.4 us
    another operation x18, other arithmetic, complex_solve(): factor = jnp.linalg.cholesky(normal_matrix)  74.3 us
    another operation x12, other arithmetic, complex_solve(): jax.scipy.linalg.cho_solve((factor, True), matmul(system.T, stacked))  62.8 us
    ppermute x12, starting transfers between devices, from_behind(): lax.ppermute(value, axis, [(source, source + steps) for source in range(f...  52.5 us
    all_gather x1, blocking collectives, shards(): lax.all_gather(y_interior, 'pole', axis=1, tiled=True)  47.9 us
    ppermute x12, waiting for transfers between devices, from_behind(): lax.ppermute(value, axis, [(source, source + steps) for source in range(f...  34.6 us
    dot_general x76, matrix products, matmul(): return jnp.matmul(left_side, right_side, precision=precise_mode)  23.1 us
  transfers between devices with their start and end apart: 14, of which 12 were waited for; matrix products, arithmetic and copies ran while one was open for 4% of the time, Pallas kernels for 0%

commit v1 on v0

v1 whole, which is shorter than its diff:
```python
import jax
import jax.numpy as jnp
from jax import lax
from jax.experimental import pallas as pl
from jax.experimental.pallas import tpu as pltpu
from jax.sharding import PartitionSpec as P

F32 = jnp.float32
EXACT = lax.Precision.HIGHEST


def mm(a, b):
    return lax.dot_general(a, b, (((1,), (0,)), ((), ())), precision=EXACT, preferred_element_type=F32)


def mm_nt(a, b):
    return lax.dot_general(a, b, (((1,), (1,)), ((), ())), precision=EXACT, preferred_element_type=F32)


def low_lanes(shape):
    return lax.broadcasted_iota(jnp.int32, shape, 1) < shape[1] // 2


def swap(x):
    return pltpu.roll(x, x.shape[1] // 2, 1)


def inverse(a):
    n = a.shape[0]
    lane = lax.broadcasted_iota(jnp.int32, (8, 2 * n), 1)
    sub = lax.broadcasted_iota(jnp.int32, (8, 2 * n), 0)
    sign = jnp.where(lane < n, -1.0, 1.0).astype(F32)
    tiles = [a[8 * t : 8 * t + 8, :] for t in range(n // 8)]

    def col(x, c):
        return jnp.broadcast_to(x[:, c : c + 1], (8, 2 * n))

    def row(x, j):
        return jnp.broadcast_to(x[j : j + 1, :], (8, 2 * n))

    for kb in range(n // 8):
        k0 = 8 * kb
        dr = [col(tiles[kb], k0 + j) for j in range(8)]
        di = [col(tiles[kb], n + k0 + j) for j in range(8)]
        in_re = (lane >= k0) & (lane < k0 + 8)
        in_im = (lane >= n + k0) & (lane < n + k0 + 8)
        panel = jnp.where(in_re, jnp.where(sub == lane - k0, 1.0, 0.0), jnp.where(in_im, 0.0, tiles[kb]))
        turned = pltpu.roll(panel, n, 1) * sign
        others = [t for t in range(n // 8) if t != kb]
        cr = {t: [col(tiles[t], k0 + j) for j in range(8)] for t in others}
        ci = {t: [col(tiles[t], n + k0 + j) for j in range(8)] for t in others}
        for j in range(8):
            me = sub == j
            pr, pi = row(dr[j], j), row(di[j], j)
            size = 1.0 / (pr * pr + pi * pi)
            qr, qi = pr * size, -pi * size
            for m in range(j + 1, 8):
                ar, ai = row(dr[m], j), row(di[m], j)
                tr, ti = ar * qr - ai * qi, ar * qi + ai * qr
                dr[m], di[m] = (
                    jnp.where(me, tr, dr[m] - dr[j] * tr + di[j] * ti),
                    jnp.where(me, ti, di[m] - dr[j] * ti - di[j] * tr),
                )
            pj, tj = row(panel, j), row(turned, j)
            s, sx = pj * qr + tj * qi, tj * qr - pj * qi
            panel, turned = (
                jnp.where(me, s, panel - dr[j] * s - di[j] * sx),
                jnp.where(me, sx, turned - dr[j] * sx + di[j] * s),
            )
        tiles[kb] = panel
        rows = [row(panel, j) for j in range(8)]
        turns = [row(turned, j) for j in range(8)]
        for t in others:
            b = jnp.where(in_re | in_im, 0.0, tiles[t])
            for j in range(8):
                b = b - cr[t][j] * rows[j] - ci[t][j] * turns[j]
            tiles[t] = b
    return jnp.concatenate(tiles, axis=0)


def embed(a):
    low = low_lanes(a.shape)
    return jnp.concatenate([jnp.where(low, a, -a), swap(a)], axis=0)


def embed_pair(x):
    n = x.shape[0] // 2
    top, bot = x[:n], x[n:]
    low = low_lanes(top.shape)
    st, sb = swap(top), swap(bot)
    first = jnp.concatenate([jnp.where(low, top, -sb), jnp.where(low, bot, st)], axis=0)
    second = jnp.concatenate([jnp.where(low, st, -bot), jnp.where(low, sb, top)], axis=0)
    return first, second


def kernel_call(body, outs, *args, smem=0, name=None):
    spaces = [pltpu.VMEM] * (len(args) - smem) + [pltpu.SMEM] * smem
    return pl.pallas_call(
        body,
        out_shape=[jax.ShapeDtypeStruct(o, F32) for o in outs],
        in_specs=[pl.BlockSpec(memory_space=m) for m in spaces],
        out_specs=[pl.BlockSpec(memory_space=pltpu.VMEM)] * len(outs),
        name=name,
    )(*args)


def condense_body(g_ref, map_ref, rows_ref, sep_ref, pole_ref, vt_ref, k_ref):
    n = g_ref.shape[1]
    s = sep_ref.shape[0]
    spread = []
    for side in range(2):
        where = rows_ref[side : side + 1, :]
        hot = (lax.broadcasted_iota(jnp.int32, (n, where.shape[1]), 0) == where).astype(F32)
        spread.append(mm_nt(map_ref[side], hot))
    both = jnp.concatenate(spread, axis=0)
    ones = lax.broadcasted_iota(jnp.int32, (s, s), 0) == lax.broadcasted_iota(jnp.int32, (s, s), 1)
    for part in range(2):
        vt = mm(both, g_ref[part])
        vt_ref[2 * s * part : 2 * s * (part + 1), :] = vt
        k_ref[2 * s * part : 2 * s * (part + 1), :] = mm_nt(vt, both)
        shift = jnp.where(ones, pole_ref[part], 0.0)
        own = sep_ref[...] - shift if part == 0 else -shift
        k_ref[2 * s * part : 2 * s * part + s, :s] += own


def rights_body(vt_ref, y_ref, ysep_ref, r_ref):
    s = ysep_ref.shape[0]
    r_ref[...] = mm(vt_ref[...], y_ref[...])
    r_ref[:s, :] += ysep_ref[...]


def merge_body(mine_ref, his_ref, rm_ref, rh_ref, flag_ref, k_ref, r_ref, w_ref, v_ref):
    first = flag_ref[0] == 0
    s = k_ref.shape[0] // 4

    def pick(x, y):
        return jnp.where(first, x, y), jnp.where(first, y, x)

    ka, kb = pick(mine_ref[...], his_ref[...])
    ra, rb = pick(rm_ref[...], rh_ref[...])
    aer, afr, aei, afi = (ka[i * s : (i + 1) * s] for i in range(4))
    ber, bfr, bei, bfi = (kb[i * s : (i + 1) * s] for i in range(4))
    low = low_lanes((s, 2 * s))
    pivot = -jnp.where(low, aer + swap(bfr), swap(aei) + bfi)
    inv = embed(inverse(pivot))
    near = jnp.concatenate([jnp.where(low, bfr, aer), jnp.where(low, bfi, aei)], axis=0)
    right = jnp.concatenate([ra[:s] + rb[s : 2 * s], ra[2 * s : 3 * s] + rb[3 * s :]], axis=0)
    w, v = mm(inv, near), mm(inv, right)
    w_ref[...] = w
    v_ref[...] = v
    far = jnp.concatenate(
        [
            jnp.where(low, swap(ber), -bei),
            jnp.where(low, afr, -swap(afi)),
            jnp.where(low, swap(bei), ber),
            jnp.where(low, afi, swap(afr)),
        ],
        axis=0,
    )
    base = jnp.concatenate(
        [jnp.where(low, ber, 0.0), jnp.where(low, 0.0, afr), jnp.where(low, bei, 0.0), jnp.where(low, 0.0, afi)], axis=0
    )
    k_ref[...] = base + mm(far, w)
    rest = jnp.concatenate([rb[:s], ra[s : 2 * s], rb[2 * s : 3 * s], ra[3 * s :]], axis=0)
    r_ref[...] = rest + mm(far, v)


def open_body(k_ref, r_ref, kn_ref, rn_ref, flag_ref, p_ref, n_ref, q_ref, w_ref, v_ref):
    s = p_ref.shape[0]
    k, kn, r = k_ref[...], kn_ref[...], r_ref[...]
    er, ei = k[:s], k[2 * s : 3 * s]
    fr, fi = kn[:s], kn[s:]
    low = low_lanes((s, 2 * s))
    pivot = -jnp.where(low, er + swap(fr), swap(ei) + fi)
    left = jnp.where(flag_ref[0] == 0, 0.0, 1.0)
    near = jnp.concatenate([jnp.where(low, fr, er * left), jnp.where(low, fi, ei * left)], axis=0)
    right = jnp.concatenate([r[:s], r[2 * s : 3 * s]], axis=0) + rn_ref[...]
    inv = embed(inverse(pivot))
    p_ref[...] = pivot
    n_ref[...] = near
    q_ref[...] = right
    w_ref[...] = mm(inv, near)
    v_ref[...] = mm(inv, right)


def level_step(p_ref, n_ref, q_ref, wu_ref, vu_ref, wd_ref, vd_ref):
    s = p_ref.shape[0]
    up, down = embed_pair(n_ref[...])
    a, b = mm(up, wu_ref[...]), mm(down, wd_ref[...])
    low = low_lanes(a.shape)
    d = jnp.where(low, b, a)
    d = d + swap(d)
    pivot = p_ref[...] - jnp.where(low[:s], d[:s], d[s:])
    right = q_ref[...] + mm(up, vu_ref[...]) + mm(down, vd_ref[...])
    return pivot, jnp.where(low, a, b), right


def level_body(p_ref, n_ref, q_ref, wu_ref, vu_ref, wd_ref, vd_ref, po_ref, no_ref, qo_ref, w_ref, v_ref):
    pivot, near, right = level_step(p_ref, n_ref, q_ref, wu_ref, vu_ref, wd_ref, vd_ref)
    inv = embed(inverse(pivot))
    po_ref[...] = pivot
    no_ref[...] = near
    qo_ref[...] = right
    w_ref[...] = mm(inv, near)
    v_ref[...] = mm(inv, right)


def last_body(p_ref, n_ref, q_ref, wu_ref, vu_ref, wd_ref, vd_ref, s_ref):
    pivot, _, right = level_step(p_ref, n_ref, q_ref, wu_ref, vu_ref, wd_ref, vd_ref)
    s_ref[...] = mm(embed(inverse(pivot)), right)


def back_body(w_ref, v_ref, after_ref, before_ref, s_ref):
    one, two = embed_pair(w_ref[...])
    s_ref[...] = v_ref[...] + mm(one, after_ref[...]) + mm(two, before_ref[...])


def field_body(g_ref, vt_ref, y_ref, after_ref, before_ref, pole_ref, f_ref, fs_ref):
    s = fs_ref.shape[0]
    wr, wi = pole_ref[2], pole_ref[3]
    after, before, y = after_ref[...], before_ref[...], y_ref[...]
    real = [wr * x[:s] - wi * x[s:] for x in (after, before)]
    imag = [-wr * x[s:] - wi * x[:s] for x in (after, before)]
    fs_ref[...] = real[0]
    sol = jnp.concatenate(real + imag, axis=0)
    f_ref[...] = (
        mm(g_ref[0], wr * y)
        - mm(g_ref[1], wi * y)
        + lax.dot_general(vt_ref[...], sol, (((0,), (0,)), ((), ())), precision=EXACT, preferred_element_type=F32)
    )


def gather_rows(y, groups_z, groups_x):
    rows, cols = y.shape
    a = jnp.broadcast_to(y[None], (4, rows, cols))
    a = lax.all_to_all(a, "pole", 0, 0, tiled=True, axis_index_groups=groups_z)
    b = jnp.broadcast_to(a[None], (4, 4, rows, cols))
    b = lax.all_to_all(b, "pole", 0, 0, tiled=True, axis_index_groups=groups_x)
    return b.transpose(1, 0, 2, 3).reshape(16 * rows, cols)


def scatter_sum(field, sep, groups_z, groups_x):
    nf, ns, half = field.shape[0] // 16, sep.shape[0] // 16, field.shape[1] // 2
    f = field.reshape(4, 4, nf, 2, half).transpose(1, 0, 3, 2, 4).reshape(4, 4, 2 * nf, half)
    p = sep.reshape(4, 4, ns, 2, half).transpose(1, 0, 3, 2, 4).reshape(4, 4, 2 * ns, half)
    a = jnp.concatenate([f, p], axis=2)
    a = lax.all_to_all(a, "pole", 0, 0, tiled=True, axis_index_groups=groups_x).sum(0)
    a = lax.all_to_all(a, "pole", 0, 0, tiled=True, axis_index_groups=groups_z).sum(0)
    f = a[: 2 * nf].reshape(2, nf, half).transpose(1, 0, 2).reshape(nf, 2 * half)
    p = a[2 * nf :].reshape(2, ns, half).transpose(1, 0, 2).reshape(ns, 2 * half)
    return f, p


def hop(x, pairs):
    return lax.ppermute(x, "dom", pairs)


def shards(y_interior, y_separator, green, pole_data, coupling, sep_block, iface_rows):
    poles, doms = lax.axis_size("pole"), lax.axis_size("dom")
    g = green[:, 0, 0]
    pole = pole_data[:, 0]
    s, cols = y_separator.shape[1], y_separator.shape[2]
    groups_z = [[x + 4 * z for z in range(4)] for x in range(4)]
    groups_x = [[x + 4 * z for x in range(4)] for z in range(4)]
    y = y_interior[0] if poles == 1 else gather_rows(y_interior[0], groups_z, groups_x)
    me = lax.axis_index("dom")
    core, side, line = me % 2, (me // 2) % 2, me // 4
    core_flag, side_flag, line_flag = (v.astype(jnp.int32)[None] for v in (core, side, line))
    swap_core = [(i, i ^ 1) for i in range(doms)]
    swap_side = [(i, i ^ 2) for i in range(doms)]

    def shift(k):
        return [(i, i + k) for i in range(max(0, -k), doms - max(0, k))]

    vt, k0 = kernel_call(
        condense_body, [(4 * s, g.shape[1]), (4 * s, 2 * s)], g, coupling[0], iface_rows[0], sep_block[0], pole, smem=1, name="condense"
    )
    (r0,) = kernel_call(rights_body, [(4 * s, cols)], vt, y, y_separator[0], name="rights")

    half = cols // 2
    mine = jnp.where(core == 0, r0[:, :half], r0[:, half:])
    sent = jnp.where(core == 0, r0[:, half:], r0[:, :half])
    got = hop(jnp.concatenate([k0, sent], axis=1), swap_core)
    k1, r1, w1, v1 = kernel_call(
        merge_body, [(4 * s, 2 * s), (4 * s, half), (2 * s, 2 * s), (2 * s, half)],
        k0, got[:, : 2 * s], mine, got[:, 2 * s :], core_flag, smem=1, name="merge_core",
    )

    quarter = half // 2
    mine = jnp.where(side == 0, r1[:, :quarter], r1[:, quarter:])
    sent = jnp.where(side == 0, r1[:, quarter:], r1[:, :quarter])
    k_part = jnp.where(core == 0, k1[: 2 * s], k1[2 * s :])
    got = hop(jnp.concatenate([k_part, jnp.concatenate([sent[: 2 * s], sent[2 * s :]], axis=1)], axis=0), swap_side)
    other = hop(got[: 2 * s], swap_core)
    k_his = jnp.concatenate(
        [jnp.where(core == 0, got[: 2 * s], other), jnp.where(core == 0, other, got[: 2 * s])], axis=0
    )
    r_his = jnp.concatenate([got[2 * s :, :quarter], got[2 * s :, quarter:]], axis=0)
    k2, r2, w2, v2 = kernel_call(
        merge_body, [(4 * s, 2 * s), (4 * s, quarter), (2 * s, 2 * s), (2 * s, quarter)],
        k1, k_his, mine, r_his, side_flag, smem=1, name="merge_side",
    )

    k_before = jnp.concatenate([k2[s : 2 * s], k2[3 * s :]], axis=0)
    r_before = jnp.concatenate([r2[s : 2 * s], r2[3 * s :]], axis=0)
    got = hop(jnp.concatenate([k_before, r_before], axis=1), shift(-4))
    sizes = [(s, 2 * s), (2 * s, 2 * s), (2 * s, quarter), (2 * s, 2 * s), (2 * s, quarter)]
    p, n, q, w, v = kernel_call(
        open_body, sizes, k2, r2, got[:, : 2 * s], got[:, 2 * s :], line_flag, smem=1, name="open"
    )
    stride = 4
    while True:
        pack = jnp.concatenate([w, v], axis=1)
        up, down = hop(pack, shift(-stride)), hop(pack, shift(stride))
        args = (p, n, q, up[:, : 2 * s], up[:, 2 * s :], down[:, : 2 * s], down[:, 2 * s :])
        stride *= 2
        if stride >= doms:
            break
        p, n, q, w, v = kernel_call(level_body, sizes, *args, name="level")
    (after,) = kernel_call(last_body, [(2 * s, quarter)], *args, name="last")
    before = hop(after, shift(4))

    (middle,) = kernel_call(back_body, [(2 * s, quarter)], w2, v2, after, before, name="back_side")
    left, right = jnp.concatenate([middle, before], axis=1), jnp.concatenate([after, middle], axis=1)
    mine, sent = jnp.where(side == 0, left, right), jnp.where(side == 0, right, left)
    got = hop(sent, swap_side)
    after, before = (
        jnp.where(side == 0, jnp.concatenate([a, b], axis=1), jnp.concatenate([b, a], axis=1))
        for a, b in ((mine[:, :quarter], got[:, :quarter]), (mine[:, quarter:], got[:, quarter:]))
    )
    (middle,) = kernel_call(back_body, [(2 * s, half)], w1, v1, after, before, name="back_core")
    left, right = jnp.concatenate([middle, before], axis=1), jnp.concatenate([after, middle], axis=1)
    mine, sent = jnp.where(core == 0, left, right), jnp.where(core == 0, right, left)
    got = hop(sent, swap_core)
    after, before = (
        jnp.where(core == 0, jnp.concatenate([a, b], axis=1), jnp.concatenate([b, a], axis=1))
        for a, b in ((mine[:, :half], got[:, :half]), (mine[:, half:], got[:, half:]))
    )
    field, sep = kernel_call(
        field_body, [(g.shape[1], cols), (s, cols)], g, vt, y, after, before, pole, smem=1, name="field"
    )
    if poles > 1:
        field, sep = scatter_sum(field, sep, groups_z, groups_x)
    return field[None], sep[None]


def solution(mesh):
    return jax.shard_map(
        shards,
        mesh=mesh,
        in_specs=(
            P("dom", "pole", None),
            P("dom", None, None),
            P(None, "pole", "dom", None, None),
            P(None, "pole"),
            P("dom", None, None, None),
            P("dom", None, None),
            P("dom", None, None),
        ),
        out_specs=(P("dom", "pole", None), P("dom", "pole", None)),
        check_vma=False,
    )
```

time: 592 us -> 210 us (0.35)
  the two profiles are of different devices: /device:TPU:16 before, /device:TPU:8 now
where the time goes in v1:
time: 210 us; the launch traced here: 209 us
  starting transfers between devices  48.5 us (23%)
  Pallas kernels  47.8 us (23%)
  waiting for transfers between devices  41.7 us (20%)
  blocking collectives  37.3 us (18%)
  local copies, waits for them, and re-layouts  22.3 us (11%)
  other arithmetic  10 us (5%)
    pallas_call x11, Pallas kernels, kernel_call(): pl.pallas_call(body, out_shape=[jax.ShapeDtypeStruct(o, F32) for o in out...  47.8 us
    ppermute x13, starting transfers between devices, hop(): return lax.ppermute(x, 'dom', pairs)  44.2 us
    ppermute x13, waiting for transfers between devices, hop(): return lax.ppermute(x, 'dom', pairs)  38.4 us
    all_to_all x1, blocking collectives, scatter_sum(): lax.all_to_all(a, 'pole', 0, 0, tiled=True, axis_index_groups=groups_x)  13.2 us
    all_to_all x1, blocking collectives, gather_rows(): a = lax.all_to_all(a, 'pole', 0, 0, tiled=True, axis_index_groups=groups_z)  13.1 us
    all_to_all x1, blocking collectives, scatter_sum(): lax.all_to_all(a, 'pole', 0, 0, tiled=True, axis_index_groups=groups_z)  11 us
    all_to_all x1, starting transfers between devices, gather_rows(): b = lax.all_to_all(b, 'pole', 0, 0, tiled=True, axis_index_groups=groups_x)  4.29 us
  transfers between devices with their start and end apart: 14, of which 14 were waited for; matrix products, arithmetic and copies ran while one was open for 2% of the time, Pallas kernels for 2%

profile of v1, /device:TPU:8, one launch (start us, length us, event | category | flops | bytes accessed | tf_op | source)
XLA Modules:
  0.0 208.5 jit_solution(15719249715482206927)
XLA Ops:
  1.4 13.1 %all_to_all.20 = f32[4,32,256]{2,1,0:T(8,128)S(1)} all-to-all(f32[4,32,256]{2,1,0:T(8,128)S(1)} %broadcast_in_dim.23), channel_id=1, replica_groups={{0,128,256,384},{32,160,288,416},{64,192,320,448},{96,224,352,480},{1,1..., dimensions={0} | all-to-all | bytes 262144 | tf_op jit(solution)/shard_map/all_to_all | solution.py:236
  15.4 4.3 %all-to-all-start.1 = ((f32[4,4,32,256]{3,2,1,0:T(8,128)}), f32[4,4,32,256]{3,2,1,0:T(8,128)S(1)}, u32[]{:S(2)}, u32[]{:S(2)}) async-start(f32[4,4,32,256]{3,2,1,0:T(8,128)} %broadcast_in_dim.24), calls=%async_computation.1 | async-start | bytes 1048576 | tf_op jit(solution)/shard_map/all_to_all | solution.py:238
  19.7 4.7 %condense.1 = (f32[256,512]{1,0:T(8,128)}, f32[256,128]{1,0:T(8,128)}) custom-call(f32[2,512,512]{2,1,0:T(8,128)} %bitcast.26, f32[2,64,128]{2,1,0:T(8,128)} %bitcast.34, s32[2,128]{1,0:T(2,128)} %bitcast.41, f32[64,64]{1,0:T(8,128)} %bitcast.36, f32[4]{0:T(128)} %bitcast.39), custom_call_target="tpu_custom_call" | custom-call | tf_op jit(solution)/shard_map/condense/pallas_call | solution.py:98
  24.4 3.3 %all-to-all-done.1 = f32[4,4,32,256]{3,2,1,0:T(8,128)S(1)} async-done(((f32[4,4,32,256]{3,2,1,0:T(8,128)}), f32[4,4,32,256]{3,2,1,0:T(8,128)S(1)}, u32[]{:S(2)}, u32[]{:S(2)}) %all-to-all-start.1) | async-done | bytes 524320 | tf_op jit(solution)/shard_map/all_to_all | solution.py:238
  28.6 2.6 %rights.1 = f32[256,256]{1,0:T(8,128)} custom-call(f32[256,512]{1,0:T(8,128)} %get-tuple-element.29.vt_ref, f32[512,256]{1,0:T(8,128)} %bitcast.28, f32[64,256]{1,0:T(8,128)} %bitcast.35), custom_call_target="tpu_custom_call" | custom-call | tf_op jit(solution)/shard_map/rights/pallas_call | solution.py:98
  32.8 1.9 collective-permute-start
  37.0 5.4 %merge_core.1 = (f32[256,128]{1,0:T(8,128)}, f32[256,128]{1,0:T(8,128)}, f32[128,128]{1,0:T(8,128)}, f32[128,128]{1,0:T(8,128)}) custom-call(f32[256,128]{1,0:T(8,128)} %get-tuple-element.30.mine_ref, f32[256,128]{1,0:T(8,128)} %get-tuple-element.57.his_ref, f32[256,128]{1,0:T(8,128)} %get-tuple-element.58.rm_ref, f32[256,128]{1,0:T(8,128)} %get-tuple-element.56.rh_ref, ...), custom_call_target="tpu_custom_call" | custom-call | tf_op jit(solution)/shard_map/merge_core/pallas_call | solution.py:98
  45.1 8.2 %collective-permute-start.1 = (f32[256,128]{1,0:T(8,128)S(1)}, f32[256,128]{1,0:T(8,128)S(1)}, u32[]{:S(2)}, u32[]{:S(2)}) collective-permute-start(f32[256,128]{1,0:T(8,128)S(1)} %maximum_maximum_fusion), channel_id=1, source_target_pairs={{0,2},{1,3},{2,0},{3,1},{4,6},{5,7},{6,4},{7,5},{8,10},{9,11},{10,... | collective-permute-start | bytes 393224 | tf_op jit(solution)/shard_map/ppermute | solution.py:255
  53.3 3.9 %collective-permute-done.1 = f32[256,128]{1,0:T(8,128)S(1)} collective-permute-done((f32[256,128]{1,0:T(8,128)S(1)}, f32[256,128]{1,0:T(8,128)S(1)}, u32[]{:S(2)}, u32[]{:S(2)}) %collective-permute-start.1) | collective-permute-done | bytes 131104 | tf_op jit(solution)/shard_map/ppermute | solution.py:255
  57.2 1.9 collective-permute-start.2
  61.0 5.4 %merge_side.1 = (f32[256,128]{1,0:T(8,128)}, f32[256,64]{1,0:T(8,128)}, f32[128,128]{1,0:T(8,128)}, f32[128,64]{1,0:T(8,128)}) custom-call(f32[256,128]{1,0:T(8,128)} %get-tuple-element.33.mine_ref, f32[256,128]{1,0:T(8,128)} %pad_maximum_fusion.2.his_ref, f32[256,64]{1,0:T(8,128)} %get-tuple-element.76.rm_ref, f32[256,64]{1,0:T(8,128)} %pad_maximum_fusion.3.rh_ref, ...), custom_call_target="tpu_custom_call" | custom-call | tf_op jit(solution)/shard_map/merge_side/pallas_call | solution.py:98
  68.0 2.5 %collective-permute-start.3 = (f32[128,192]{1,0:T(8,128)S(1)}, f32[128,192]{1,0:T(8,128)S(1)}, u32[]{:S(2)}, u32[]{:S(2)}) collective-permute-start(f32[128,192]{1,0:T(8,128)S(1)} %maximum_maximum_fusion.1), channel_id=1, source_target_pairs={{4,0},{5,1},{6,2},{7,3},{8,4},{9,5},{10,6},{11,7},{12,8},{13,9},{1... | collective-permute-start | bytes 294920 | tf_op jit(solution)/shard_map/ppermute | solution.py:255
  70.5 4.9 %collective-permute-done.3 = f32[128,192]{1,0:T(8,128)S(1)} collective-permute-done((f32[128,192]{1,0:T(8,128)S(1)}, f32[128,192]{1,0:T(8,128)S(1)}, u32[]{:S(2)}, u32[]{:S(2)}) %collective-permute-start.3) | collective-permute-done | bytes 98336 | tf_op jit(solution)/shard_map/ppermute | solution.py:255
  76.7 5.2 %open.1 = (f32[64,128]{1,0:T(8,128)}, f32[128,128]{1,0:T(8,128)}, f32[128,64]{1,0:T(8,128)}, f32[128,128]{1,0:T(8,128)}, f32[128,64]{1,0:T(8,128)}) custom-call(f32[256,128]{1,0:T(8,128)} %get-tuple-element.37.k_ref, f32[256,64]{1,0:T(8,128)} %get-tuple-element.38.r_ref, f32[128,128]{1,0:T(8,128)} %slice.179.kn_ref, f32[128,64]{1,0:T(8,128)} %slice.180.rn_ref, ...), custom_call_target="tpu_custom_call" | custom-call | tf_op jit(solution)/shard_map/open/pallas_call | solution.py:98
  83.6 3.5 %collective-permute-start.5 = (f32[128,192]{1,0:T(8,128)S(1)}, f32[128,192]{1,0:T(8,128)S(1)}, u32[]{:S(2)}, u32[]{:S(2)}) collective-permute-start(f32[128,192]{1,0:T(8,128)S(1)} %constant_dynamic-update-slice_fusion), channel_id=1, source_target_pairs={{0,4},{1,5},{2,6},{3,7},{4,8},{5,9},{6,10},{7,11},{8,12},{9,13},{1... | collective-permute-start | bytes 294920 | tf_op jit(solution)/shard_map/ppermute | solution.py:255
  87.1 2.3 %collective-permute-start.4 = (f32[128,192]{1,0:T(8,128)S(1)}, f32[128,192]{1,0:T(8,128)S(1)}, u32[]{:S(2)}, u32[]{:S(2)}) collective-permute-start(f32[128,192]{1,0:T(8,128)S(1)} %constant_dynamic-update-slice_fusion), channel_id=1, source_target_pairs={{4,0},{5,1},{6,2},{7,3},{8,4},{9,5},{10,6},{11,7},{12,8},{13,9},{1... | collective-permute-start | bytes 294920 | tf_op jit(solution)/shard_map/ppermute | solution.py:255
  91.7 3.0 %collective-permute-done.4 = f32[128,192]{1,0:T(8,128)S(1)} collective-permute-done((f32[128,192]{1,0:T(8,128)S(1)}, f32[128,192]{1,0:T(8,128)S(1)}, u32[]{:S(2)}, u32[]{:S(2)}) %collective-permute-start.4) | collective-permute-done | bytes 98336 | tf_op jit(solution)/shard_map/ppermute | solution.py:255
  96.0 5.2 %level.2 = (f32[64,128]{1,0:T(8,128)}, f32[128,128]{1,0:T(8,128)}, f32[128,64]{1,0:T(8,128)}, f32[128,128]{1,0:T(8,128)}, f32[128,64]{1,0:T(8,128)}) custom-call(f32[64,128]{1,0:T(8,128)} %get-tuple-element.39.p_ref, f32[128,128]{1,0:T(8,128)} %get-tuple-element.40.n_ref, f32[128,64]{1,0:T(8,128)} %get-tuple-element.41.q_ref, f32[128,128]{1,0:T(8,128)} %slice.181.wu_ref, ...), custom_call_target="tpu_custom_call" | custom-call | tf_op jit(solution)/shard_map/level/pallas_call | solution.py:98
  102.9 6.1 %collective-permute-start.7 = (f32[128,192]{1,0:T(8,128)S(1)}, f32[128,192]{1,0:T(8,128)S(1)}, u32[]{:S(2)}, u32[]{:S(2)}) collective-permute-start(f32[128,192]{1,0:T(8,128)S(1)} %constant_dynamic-update-slice_fusion.2), channel_id=1, source_target_pairs={{0,8},{1,9},{2,10},{3,11},{4,12},{5,13},{6,14},{7,15},{8,16},{9,17... | collective-permute-start | bytes 294920 | tf_op jit(solution)/shard_map/ppermute | solution.py:255
  112.8 5.1 %collective-permute-done.6 = f32[128,192]{1,0:T(8,128)S(1)} collective-permute-done((f32[128,192]{1,0:T(8,128)S(1)}, f32[128,192]{1,0:T(8,128)S(1)}, u32[]{:S(2)}, u32[]{:S(2)}) %collective-permute-start.6) | collective-permute-done | bytes 98336 | tf_op jit(solution)/shard_map/ppermute | solution.py:255
  119.2 5.2 %level.3 = (f32[64,128]{1,0:T(8,128)}, f32[128,128]{1,0:T(8,128)}, f32[128,64]{1,0:T(8,128)}, f32[128,128]{1,0:T(8,128)}, f32[128,64]{1,0:T(8,128)}) custom-call(f32[64,128]{1,0:T(8,128)} %get-tuple-element.44.p_ref, f32[128,128]{1,0:T(8,128)} %get-tuple-element.45.n_ref, f32[128,64]{1,0:T(8,128)} %get-tuple-element.46.q_ref, f32[128,128]{1,0:T(8,128)} %slice.185.wu_ref, ...), custom_call_target="tpu_custom_call" | custom-call | tf_op jit(solution)/shard_map/level/pallas_call | solution.py:98
  126.1 2.2 %collective-permute-start.9 = (f32[128,192]{1,0:T(8,128)S(1)}, f32[128,192]{1,0:T(8,128)S(1)}, u32[]{:S(2)}, u32[]{:S(2)}) collective-permute-start(f32[128,192]{1,0:T(8,128)S(1)} %constant_dynamic-update-slice_fusion.4), channel_id=1, source_target_pairs={{0,16},{1,17},{2,18},{3,19},{4,20},{5,21},{6,22},{7,23},{8,24},{9,... | collective-permute-start | bytes 294920 | tf_op jit(solution)/shard_map/ppermute | solution.py:255
  132.8 7.4 %collective-permute-done.8 = f32[128,192]{1,0:T(8,128)S(1)} collective-permute-done((f32[128,192]{1,0:T(8,128)S(1)}, f32[128,192]{1,0:T(8,128)S(1)}, u32[]{:S(2)}, u32[]{:S(2)}) %collective-permute-start.8) | collective-permute-done | bytes 98336 | tf_op jit(solution)/shard_map/ppermute | solution.py:255
  141.4 5.4 %last.1.after_ref = f32[128,64]{1,0:T(8,128)} custom-call(f32[64,128]{1,0:T(8,128)} %get-tuple-element.49.p_ref, f32[128,128]{1,0:T(8,128)} %get-tuple-element.50.n_ref, f32[128,64]{1,0:T(8,128)} %get-tuple-element.51.q_ref, f32[128,128]{1,0:T(8,128)} %slice.189.wu_ref, f32[128,64]{1,0:T(8,128)} %slice.190.vu_ref, f32[128,128]{1,0:T(8,128)} %slice.191.wd_ref, ...), custom_call_target="tpu_custom_call" | custom-call | tf_op jit(solution)/shard_map/last/pallas_call | solution.py:98
  146.7 1.9 collective-permute-start.10
  148.7 4.4 %collective-permute-done.10.before_ref = f32[128,64]{1,0:T(8,128)S(1)} collective-permute-done((f32[128,64]{1,0:T(8,128)}, f32[128,64]{1,0:T(8,128)S(1)}, u32[]{:S(2)}, u32[]{:S(2)}) %collective-permute-start.10) | collective-permute-done | bytes 32800 | tf_op jit(solution)/shard_map/ppermute | solution.py:255
  156.6 8.8 %collective-permute-start.11 = (f32[128,128]{1,0:T(8,128)S(1)}, f32[128,128]{1,0:T(8,128)S(1)}, u32[]{:S(2)}, u32[]{:S(2)}) collective-permute-start(f32[128,128]{1,0:T(8,128)S(1)} %get-tuple-element.63), channel_id=1, source_target_pairs={{0,2},{1,3},{2,0},{3,1},{4,6},{5,7},{6,4},{7,5},{8,10},{9,11},{10,... | collective-permute-start | bytes 196616 | tf_op jit(solution)/shard_map/ppermute | solution.py:255
  165.5 2.6 %collective-permute-done.11 = f32[128,128]{1,0:T(8,128)S(1)} collective-permute-done((f32[128,128]{1,0:T(8,128)S(1)}, f32[128,128]{1,0:T(8,128)S(1)}, u32[]{:S(2)}, u32[]{:S(2)}) %collective-permute-start.11) | collective-permute-done | bytes 65568 | tf_op jit(solution)/shard_map/ppermute | solution.py:255
  172.5 1.9 collective-permute-start.12
  176.5 5.0 %field.1 = (f32[512,256]{1,0:T(8,128)}, f32[64,256]{1,0:T(8,128)}) custom-call(f32[2,512,512]{2,1,0:T(8,128)} %bitcast.27, f32[256,512]{1,0:T(8,128)} %get-tuple-element.29.vt_ref, f32[512,256]{1,0:T(8,128)} %bitcast.29, f32[128,256]{1,0:T(8,128)} %get-tuple-element.84.after_ref, f32[128,256]{1,0:T(8,128)} %get-tuple-element.85.before_ref, f32[4]{0:T(128)} %bitcast.40), custom_call_target="tpu_custom_call" | custom-call | tf_op jit(solution)/shard_map/field/pallas_call | solution.py:98
  183.1 13.2 %all_to_all.21 = f32[4,4,72,128]{3,2,1,0:T(8,128)S(1)} all-to-all(f32[4,4,72,128]{3,2,1,0:T(8,128)S(1)} %pad_maximum_fusion), channel_id=1, replica_groups={{0,32,64,96},{128,160,192,224},{256,288,320,352},{384,416,448,480},{1,3..., dimensions={0} | all-to-all | bytes 1179648 | tf_op jit(solution)/shard_map/all_to_all | solution.py:247
  196.3 11.0 %all_to_all.22 = f32[4,72,128]{2,1,0:T(8,128)S(1)} all-to-all(f32[4,72,128]{2,1,0:T(8,128)S(1)} %reduce_sum.18), channel_id=1, replica_groups={{0,128,256,384},{32,160,288,416},{64,192,320,448},{96,224,352,480},{1,1..., dimensions={0} | all-to-all | bytes 294912 | tf_op jit(solution)/shard_map/all_to_all | solution.py:248
  (74 shorter events, 46.0 us)
Async XLA Ops:
  15.4 12.4 %all-to-all-start.1 = ((f32[4,4,32,256]{3,2,1,0:T(8,128)}), f32[4,4,32,256]{3,2,1,0:T(8,128)S(1)}, u32[]{:S(2)}, u32[]{:S(2)}) async-start(f32[4,4,32,256]{3,2,1,0:T(8,128)} %broadcast_in_dim.24), calls=%async_computation.1 | async-start | bytes 1048576 | tf_op jit(solution)/shard_map/all_to_all | solution.py:238
  24.4 8.4 %copy-start = (f32[256,128]{1,0:T(8,128)S(1)}, f32[256,128]{1,0:T(8,128)}, u32[]{:S(2)}) copy-start(f32[256,128]{1,0:T(8,128)} %get-tuple-element.30.mine_ref) | copy-start | bytes 393220
  32.8 3.4 %collective-permute-start = (f32[256,256]{1,0:T(8,128)S(1)}, f32[256,256]{1,0:T(8,128)S(1)}, u32[]{:S(2)}, u32[]{:S(2)}) collective-permute-start(f32[256,256]{1,0:T(8,128)S(1)} %pad_maximum_fusion.1), channel_id=1, source_target_pairs={{0,1},{1,0},{2,3},{3,2},{4,5},{5,4},{6,7},{7,6},{8,9},{9,8},{10,11... | collective-permute-start | bytes 786440 | tf_op jit(solution)/shard_map/ppermute | solution.py:255
  45.1 12.1 %collective-permute-start.1 = (f32[256,128]{1,0:T(8,128)S(1)}, f32[256,128]{1,0:T(8,128)S(1)}, u32[]{:S(2)}, u32[]{:S(2)}) collective-permute-start(f32[256,128]{1,0:T(8,128)S(1)} %maximum_maximum_fusion), channel_id=1, source_target_pairs={{0,2},{1,3},{2,0},{3,1},{4,6},{5,7},{6,4},{7,5},{8,10},{9,11},{10,... | collective-permute-start | bytes 393224 | tf_op jit(solution)/shard_map/ppermute | solution.py:255
  57.2 3.1 %collective-permute-start.2 = (f32[128,128]{1,0:T(8,128)S(1)}, f32[128,128]{1,0:T(8,128)S(1)}, u32[]{:S(2)}, u32[]{:S(2)}) collective-permute-start(f32[128,128]{1,0:T(8,128)S(1)} %slice.176), channel_id=1, source_target_pairs={{0,1},{1,0},{2,3},{3,2},{4,5},{5,4},{6,7},{7,6},{8,9},{9,8},{10,11... | collective-permute-start | bytes 196616 | tf_op jit(solution)/shard_map/ppermute | solution.py:255
  68.0 7.5 %collective-permute-start.3 = (f32[128,192]{1,0:T(8,128)S(1)}, f32[128,192]{1,0:T(8,128)S(1)}, u32[]{:S(2)}, u32[]{:S(2)}) collective-permute-start(f32[128,192]{1,0:T(8,128)S(1)} %maximum_maximum_fusion.1), channel_id=1, source_target_pairs={{4,0},{5,1},{6,2},{7,3},{8,4},{9,5},{10,6},{11,7},{12,8},{13,9},{1... | collective-permute-start | bytes 294920 | tf_op jit(solution)/shard_map/ppermute | solution.py:255
  83.6 6.8 %collective-permute-start.5 = (f32[128,192]{1,0:T(8,128)S(1)}, f32[128,192]{1,0:T(8,128)S(1)}, u32[]{:S(2)}, u32[]{:S(2)}) collective-permute-start(f32[128,192]{1,0:T(8,128)S(1)} %constant_dynamic-update-slice_fusion), channel_id=1, source_target_pairs={{0,4},{1,5},{2,6},{3,7},{4,8},{5,9},{6,10},{7,11},{8,12},{9,13},{1... | collective-permute-start | bytes 294920 | tf_op jit(solution)/shard_map/ppermute | solution.py:255
  87.1 7.6 %collective-permute-start.4 = (f32[128,192]{1,0:T(8,128)S(1)}, f32[128,192]{1,0:T(8,128)S(1)}, u32[]{:S(2)}, u32[]{:S(2)}) collective-permute-start(f32[128,192]{1,0:T(8,128)S(1)} %constant_dynamic-update-slice_fusion), channel_id=1, source_target_pairs={{4,0},{5,1},{6,2},{7,3},{8,4},{9,5},{10,6},{11,7},{12,8},{13,9},{1... | collective-permute-start | bytes 294920 | tf_op jit(solution)/shard_map/ppermute | solution.py:255
  102.9 8.7 %collective-permute-start.7 = (f32[128,192]{1,0:T(8,128)S(1)}, f32[128,192]{1,0:T(8,128)S(1)}, u32[]{:S(2)}, u32[]{:S(2)}) collective-permute-start(f32[128,192]{1,0:T(8,128)S(1)} %constant_dynamic-update-slice_fusion.2), channel_id=1, source_target_pairs={{0,8},{1,9},{2,10},{3,11},{4,12},{5,13},{6,14},{7,15},{8,16},{9,17... | collective-permute-start | bytes 294920 | tf_op jit(solution)/shard_map/ppermute | solution.py:255
  109.0 8.9 %collective-permute-start.6 = (f32[128,192]{1,0:T(8,128)S(1)}, f32[128,192]{1,0:T(8,128)S(1)}, u32[]{:S(2)}, u32[]{:S(2)}) collective-permute-start(f32[128,192]{1,0:T(8,128)S(1)} %constant_dynamic-update-slice_fusion.2), channel_id=1, source_target_pairs={{8,0},{9,1},{10,2},{11,3},{12,4},{13,5},{14,6},{15,7},{16,8},{17,9... | collective-permute-start | bytes 294920 | tf_op jit(solution)/shard_map/ppermute | solution.py:255
  126.1 5.4 %collective-permute-start.9 = (f32[128,192]{1,0:T(8,128)S(1)}, f32[128,192]{1,0:T(8,128)S(1)}, u32[]{:S(2)}, u32[]{:S(2)}) collective-permute-start(f32[128,192]{1,0:T(8,128)S(1)} %constant_dynamic-update-slice_fusion.4), channel_id=1, source_target_pairs={{0,16},{1,17},{2,18},{3,19},{4,20},{5,21},{6,22},{7,23},{8,24},{9,... | collective-permute-start | bytes 294920 | tf_op jit(solution)/shard_map/ppermute | solution.py:255
  128.3 11.8 %collective-permute-start.8 = (f32[128,192]{1,0:T(8,128)S(1)}, f32[128,192]{1,0:T(8,128)S(1)}, u32[]{:S(2)}, u32[]{:S(2)}) collective-permute-start(f32[128,192]{1,0:T(8,128)S(1)} %constant_dynamic-update-slice_fusion.4), channel_id=1, source_target_pairs={{16,0},{17,1},{18,2},{19,3},{20,4},{21,5},{22,6},{23,7},{24,8},{25... | collective-permute-start | bytes 294920 | tf_op jit(solution)/shard_map/ppermute | solution.py:255
  146.7 6.4 %collective-permute-start.10 = (f32[128,64]{1,0:T(8,128)}, f32[128,64]{1,0:T(8,128)S(1)}, u32[]{:S(2)}, u32[]{:S(2)}) collective-permute-start(f32[128,64]{1,0:T(8,128)} %last.1.after_ref), channel_id=1, source_target_pairs={{0,4},{1,5},{2,6},{3,7},{4,8},{5,9},{6,10},{7,11},{8,12},{9,13},{1... | collective-permute-start | bytes 98312 | tf_op jit(solution)/shard_map/ppermute | solution.py:255
  153.1 0.6 copy-start.1
  156.6 11.5 %collective-permute-start.11 = (f32[128,128]{1,0:T(8,128)S(1)}, f32[128,128]{1,0:T(8,128)S(1)}, u32[]{:S(2)}, u32[]{:S(2)}) collective-permute-start(f32[128,128]{1,0:T(8,128)S(1)} %get-tuple-element.63), channel_id=1, source_target_pairs={{0,2},{1,3},{2,0},{3,1},{4,6},{5,7},{6,4},{7,5},{8,10},{9,11},{10,... | collective-permute-start | bytes 196616 | tf_op jit(solution)/shard_map/ppermute | solution.py:255
  172.5 3.2 %collective-permute-start.12 = (f32[128,256]{1,0:T(8,128)S(1)}, f32[128,256]{1,0:T(8,128)S(1)}, u32[]{:S(2)}, u32[]{:S(2)}) collective-permute-start(f32[128,256]{1,0:T(8,128)S(1)} %get-tuple-element.61), channel_id=1, source_target_pairs={{0,1},{1,0},{2,3},{3,2},{4,5},{5,4},{6,7},{7,6},{8,9},{9,8},{10,11... | collective-permute-start | bytes 393224 | tf_op jit(solution)/shard_map/ppermute | solution.py:255
  181.5 1.4 copy-start.2

commit v2 on v1

v2 whole, which is shorter than its diff:
```python
import jax
import jax.numpy as jnp
from jax import lax
from jax.experimental import pallas as pl
from jax.experimental.pallas import tpu as pltpu
from jax.sharding import PartitionSpec as P


F32 = jnp.float32
EXACT = lax.Precision.HIGHEST


def mm(a, b):
    return lax.dot_general(a, b, (((1,), (0,)), ((), ())), precision=EXACT, preferred_element_type=F32)


def mm_nt(a, b):
    return lax.dot_general(a, b, (((1,), (1,)), ((), ())), precision=EXACT, preferred_element_type=F32)


def low_lanes(shape):
    return lax.broadcasted_iota(jnp.int32, shape, 1) < shape[1] // 2


def swap(x):
    return pltpu.roll(x, x.shape[1] // 2, 1)


def inverse(a):
    n = a.shape[0]
    lane = lax.broadcasted_iota(jnp.int32, (8, 2 * n), 1)
    sub = lax.broadcasted_iota(jnp.int32, (8, 2 * n), 0)
    sign = jnp.where(lane < n, -1.0, 1.0).astype(F32)
    tiles = [a[8 * t : 8 * t + 8, :] for t in range(n // 8)]

    def col(x, c):
        return jnp.broadcast_to(x[:, c : c + 1], (8, 2 * n))

    def row(x, j):
        return jnp.broadcast_to(x[j : j + 1, :], (8, 2 * n))

    for kb in range(n // 8):
        k0 = 8 * kb
        dr = [col(tiles[kb], k0 + j) for j in range(8)]
        di = [col(tiles[kb], n + k0 + j) for j in range(8)]
        in_re = (lane >= k0) & (lane < k0 + 8)
        in_im = (lane >= n + k0) & (lane < n + k0 + 8)
        panel = jnp.where(in_re, jnp.where(sub == lane - k0, 1.0, 0.0), jnp.where(in_im, 0.0, tiles[kb]))
        turned = pltpu.roll(panel, n, 1) * sign
        others = [t for t in range(n // 8) if t != kb]
        cr = {t: [col(tiles[t], k0 + j) for j in range(8)] for t in others}
        ci = {t: [col(tiles[t], n + k0 + j) for j in range(8)] for t in others}
        for j in range(8):
            me = sub == j
            pr, pi = row(dr[j], j), row(di[j], j)
            size = 1.0 / (pr * pr + pi * pi)
            qr, qi = pr * size, -pi * size
            for m in range(j + 1, 8):
                ar, ai = row(dr[m], j), row(di[m], j)
                tr, ti = ar * qr - ai * qi, ar * qi + ai * qr
                dr[m], di[m] = (
                    jnp.where(me, tr, dr[m] - dr[j] * tr + di[j] * ti),
                    jnp.where(me, ti, di[m] - dr[j] * ti - di[j] * tr),
                )
            pj, tj = row(panel, j), row(turned, j)
            s, sx = pj * qr + tj * qi, tj * qr - pj * qi
            panel, turned = (
                jnp.where(me, s, panel - dr[j] * s - di[j] * sx),
                jnp.where(me, sx, turned - dr[j] * sx + di[j] * s),
            )
        tiles[kb] = panel
        rows = [row(panel, j) for j in range(8)]
        turns = [row(turned, j) for j in range(8)]
        for t in others:
            b = jnp.where(in_re | in_im, 0.0, tiles[t])
            for j in range(8):
                b = b - cr[t][j] * rows[j] - ci[t][j] * turns[j]
            tiles[t] = b
    return jnp.concatenate(tiles, axis=0)


def embed(a):
    low = low_lanes(a.shape)
    return jnp.concatenate([jnp.where(low, a, -a), swap(a)], axis=0)


def embed_pair(x):
    n = x.shape[0] // 2
    top, bot = x[:n], x[n:]
    low = low_lanes(top.shape)
    st, sb = swap(top), swap(bot)
    first = jnp.concatenate([jnp.where(low, top, -sb), jnp.where(low, bot, st)], axis=0)
    second = jnp.concatenate([jnp.where(low, st, -bot), jnp.where(low, sb, top)], axis=0)
    return first, second


def kernel_call(body, outs, *args, smem=0, us=1.0, loose=(), loose_outs=False, hbm=(), scratch=()):
    count = len(args) - smem
    args = [
        a
        if i >= count or i in loose
        else pltpu.with_memory_space_constraint(a, pltpu.HBM if i in hbm else pltpu.VMEM)
        for i, a in enumerate(args)
    ]
    return pl.pallas_call(
        body,
        out_shape=[jax.ShapeDtypeStruct(o, F32) if loose_outs else pltpu.VMEM(o, F32) for o in outs],
        cost_estimate=pl.CostEstimate(flops=int(us * 1e9), bytes_accessed=1 << 16, transcendentals=0),
        in_specs=[
            pl.BlockSpec(memory_space=pltpu.SMEM if i >= count else pltpu.HBM if i in hbm else pltpu.VMEM)
            for i in range(len(args))
        ],
        scratch_shapes=list(scratch),
        out_specs=[pl.BlockSpec(memory_space=pltpu.VMEM)] * len(outs),
        compiler_params=pltpu.CompilerParams(vmem_limit_bytes=16 << 20),
    )(*args)


def condense_body(g_hbm, map_hbm, sep_hbm, rows_ref, pole_ref, vt_ref, k_ref, g_ref, map_ref, sep_ref, sems):
    moves = [
        pltpu.make_async_copy(map_hbm, map_ref, sems.at[0]),
        pltpu.make_async_copy(g_hbm.at[0], g_ref.at[0], sems.at[1]),
        pltpu.make_async_copy(g_hbm.at[1], g_ref.at[1], sems.at[2]),
        pltpu.make_async_copy(sep_hbm, sep_ref, sems.at[3]),
    ]
    for move in moves:
        move.start()
    n = g_ref.shape[1]
    s = sep_ref.shape[0]
    spread = []
    moves[0].wait()
    for side in range(2):
        where = rows_ref[side : side + 1, :]
        hot = (lax.broadcasted_iota(jnp.int32, (n, where.shape[1]), 0) == where).astype(F32)
        spread.append(mm_nt(map_ref[side], hot))
    both = jnp.concatenate(spread, axis=0)
    ones = lax.broadcasted_iota(jnp.int32, (s, s), 0) == lax.broadcasted_iota(jnp.int32, (s, s), 1)
    for part in range(2):
        moves[1 + part].wait()
        vt = mm(both, g_ref[part])
        vt_ref[2 * s * part : 2 * s * (part + 1), :] = vt
        k_ref[2 * s * part : 2 * s * (part + 1), :] = mm_nt(vt, both)
    moves[3].wait()
    for part in range(2):
        shift = jnp.where(ones, pole_ref[part], 0.0)
        own = sep_ref[...] - shift if part == 0 else -shift
        k_ref[2 * s * part : 2 * s * part + s, :s] += own


def in_order(y_ref):
    return jnp.concatenate([y_ref[x, z] for z in range(y_ref.shape[1]) for x in range(y_ref.shape[0])], axis=0)


def rights_body(vt_ref, y_ref, ysep_ref, flag_ref, mine_ref, sent_ref):
    s, half = ysep_ref.shape[0], mine_ref.shape[1]
    r = mm(vt_ref[...], in_order(y_ref))
    r = jnp.concatenate([r[:s] + ysep_ref[...], r[s:]], axis=0)
    first = flag_ref[0] == 0
    mine_ref[...] = jnp.where(first, r[:, :half], r[:, half:])
    sent_ref[...] = jnp.where(first, r[:, half:], r[:, :half])


def join_matrices(first, ka, kb):
    s = ka.shape[0] // 4
    ka, kb = jnp.where(first, ka, kb), jnp.where(first, kb, ka)
    aer, afr, aei, afi = (ka[i * s : (i + 1) * s] for i in range(4))
    ber, bfr, bei, bfi = (kb[i * s : (i + 1) * s] for i in range(4))
    low = low_lanes((s, 2 * s))
    inv = embed(inverse(-jnp.where(low, aer + swap(bfr), swap(aei) + bfi)))
    near = jnp.concatenate([jnp.where(low, bfr, aer), jnp.where(low, bfi, aei)], axis=0)
    far = jnp.concatenate(
        [
            jnp.where(low, swap(ber), -bei),
            jnp.where(low, afr, -swap(afi)),
            jnp.where(low, swap(bei), ber),
            jnp.where(low, afi, swap(afr)),
        ],
        axis=0,
    )
    base = jnp.concatenate(
        [jnp.where(low, ber, 0.0), jnp.where(low, 0.0, afr), jnp.where(low, bei, 0.0), jnp.where(low, 0.0, afi)], axis=0
    )
    w = mm(inv, near)
    return base + mm(far, w), w, inv, far


def core_join_body(mine_ref, his_ref, core_ref, k_ref, part_ref, w_ref, inv_ref, far_ref):
    lead = core_ref[0] == 0
    k, w_ref[...], inv_ref[...], far_ref[...] = join_matrices(lead, mine_ref[...], his_ref[...])
    half = k.shape[0] // 2
    k_ref[...] = k
    part_ref[...] = jnp.where(lead, k[:half], k[half:])


def side_join_body(mine_ref, one_ref, two_ref, core_ref, flag_ref, k_ref, w_ref, inv_ref, far_ref):
    lead = core_ref[0] == 0
    one, two = one_ref[...], two_ref[...]
    his = jnp.concatenate([jnp.where(lead, one, two), jnp.where(lead, two, one)], axis=0)
    k_ref[...], w_ref[...], inv_ref[...], far_ref[...] = join_matrices(flag_ref[0] == 0, mine_ref[...], his)


def join_body(mine_ref, his_ref, flag_ref, k_ref, w_ref, inv_ref, far_ref):
    k_ref[...], w_ref[...], inv_ref[...], far_ref[...] = join_matrices(flag_ref[0] == 0, mine_ref[...], his_ref[...])


def sides_body(mine_ref, his_ref, inv_ref, far_ref, flag_ref, r_ref, v_ref):
    s = mine_ref.shape[0] // 4
    first = flag_ref[0] == 0
    mine, his = mine_ref[...], his_ref[...]
    ra, rb = jnp.where(first, mine, his), jnp.where(first, his, mine)
    v = mm(inv_ref[...], jnp.concatenate([ra[:s] + rb[s : 2 * s], ra[2 * s : 3 * s] + rb[3 * s :]], axis=0))
    v_ref[...] = v
    rest = jnp.concatenate([rb[:s], ra[s : 2 * s], rb[2 * s : 3 * s], ra[3 * s :]], axis=0)
    r_ref[...] = rest + mm(far_ref[...], v)


def end_body(k_ref, flag_ref, sent_ref, inv_ref, back_ref, fore_ref):
    s = sent_ref.shape[0]
    er, fr, ei, fi = (k_ref[i * s : (i + 1) * s, :] for i in range(4))
    low = low_lanes((s, 2 * s))
    ee = jnp.where(low, er, swap(ei))
    inv = embed(inverse(-ee))
    fore = embed(jnp.where(low, swap(er), ei))
    back = embed(jnp.where(low, fr, swap(fi)))
    inv_ref[...] = inv
    back_ref[...] = back
    through = mm(inv, fore)
    fore_ref[...] = through
    ff = jnp.where(low, swap(fr), fi)
    more = mm(back[:s], through)
    sent_ref[...] = jnp.where(flag_ref[0] == 0, ee, ff + jnp.where(low, more, -more))


def end_sides_body(r_ref, inv_ref, back_ref, flag_ref, sent_ref, v_ref):
    s = r_ref.shape[0] // 4
    e = jnp.concatenate([r_ref[:s, :], r_ref[2 * s : 3 * s, :]], axis=0)
    f = jnp.concatenate([r_ref[s : 2 * s, :], r_ref[3 * s :, :]], axis=0)
    v = mm(inv_ref[...], e)
    v_ref[...] = v
    sent_ref[...] = jnp.where(flag_ref[0] == 0, e, f + mm(back_ref[...], v))


def middle_body(mine_ref, his_ref, inv_ref):
    inv_ref[...] = embed(inverse(-(mine_ref[...] + his_ref[...])))


def back_body(*refs):
    inv_ref, mine_ref, his_ref, fore_ref, v_ref = refs[:5]
    flags, (own_ref, sent_ref) = refs[-3], refs[-2:]
    joins = refs[5:-3]
    s2 = v_ref.shape[0]
    middle = mm(inv_ref[...], mine_ref[...] + his_ref[...])
    front = flags[4] == 0
    after = jnp.where(front, middle, v_ref[...] + mm(fore_ref[...], middle))
    before = jnp.where(front, 0.0, middle)
    for level in range(3, -1, -1):
        one, two = embed_pair(joins[2 * level][...])
        middle = joins[2 * level + 1][...] + mm(
            jnp.concatenate([one, two], axis=1), jnp.concatenate([after, before], axis=0)
        )
        first = flags[level] == 0
        if level == 0:
            sent_ref[:s2, :] = jnp.where(first, after, middle)
            sent_ref[s2:, :] = jnp.where(first, middle, before)
        after, before = jnp.where(first, middle, after), jnp.where(first, before, middle)
    own_ref[:s2, :] = after
    own_ref[s2:, :] = before


def base_body(g_ref, y_ref, pole_ref, a_ref):
    y = in_order(y_ref)
    a_ref[...] = mm(g_ref[0], pole_ref[2] * y) - mm(g_ref[1], pole_ref[3] * y)


def field_body(base_ref, vt_ref, mine_ref, got_ref, pole_ref, core_ref, o_ref):
    s = mine_ref.shape[0] // 4
    wr, wi = pole_ref[2], pole_ref[3]
    lead = core_ref[0] == 0
    mine, got = mine_ref[...], got_ref[...]
    x = jnp.concatenate([jnp.where(lead, mine, got), jnp.where(lead, got, mine)], axis=1)
    re, im = [x[:s], x[2 * s : 3 * s]], [x[s : 2 * s], x[3 * s :]]
    real = [wr * a - wi * b for a, b in zip(re, im)]
    imag = [-wr * b - wi * a for a, b in zip(re, im)]
    sol = jnp.concatenate(real + imag, axis=0)
    field = base_ref[...] + lax.dot_general(
        vt_ref[...], sol, (((0,), (0,)), ((), ())), precision=EXACT, preferred_element_type=F32
    )
    nx, nz = o_ref.shape[:2]
    nf, ns, half = field.shape[0] // (nx * nz), s // (nx * nz), field.shape[1] // 2
    for i in range(nx * nz):
        z, x = divmod(i, nx)
        for h in range(2):
            o_ref[x, z, h * nf : (h + 1) * nf, :] = field[i * nf : (i + 1) * nf, h * half : (h + 1) * half]
            at = 2 * nf + h * ns
            o_ref[x, z, at : at + ns, :] = real[0][i * ns : (i + 1) * ns, h * half : (h + 1) * half]


def close_body(a_ref, f_ref, s_ref):
    a = a_ref[0]
    for i in range(1, a_ref.shape[0]):
        a = a + a_ref[i]
    nf, ns, half = f_ref.shape[0], s_ref.shape[0], a.shape[1]
    for h in range(2):
        f_ref[:, h * half : (h + 1) * half] = a[h * nf : (h + 1) * nf, :]
        s_ref[:, h * half : (h + 1) * half] = a[2 * nf + h * ns : 2 * nf + (h + 1) * ns, :]


def shards(y_interior, y_separator, green, pole_data, coupling, sep_block, iface_rows):
    doms = lax.axis_size("dom")
    g = green[:, 0, 0]
    pole = pole_data[:, 0]
    s, cols = y_separator.shape[1], y_separator.shape[2]
    rows = y_interior.shape[1]
    half = cols // 2
    groups_z = [[x + 4 * z for z in range(4)] for x in range(4)]
    groups_x = [[x + 4 * z for x in range(4)] for z in range(4)]

    def flip(x, k):
        return lax.ppermute(x, "dom", [(i, i ^ k) for i in range(doms)])

    def exchange(a, groups):
        return lax.all_to_all(a, "pole", 0, 0, tiled=True, axis_index_groups=groups)

    y = exchange(jnp.broadcast_to(y_interior[0][None], (4, rows, cols)), groups_z)
    y = exchange(jnp.broadcast_to(y[None], (4, 4, rows, cols)), groups_x)
    me = lax.axis_index("dom").astype(jnp.int32)
    flags = jnp.stack([(me >> i) & 1 for i in range(5)])
    core = flags[:1]

    big, square = (4 * s, 2 * s), (2 * s, 2 * s)
    vt, k = kernel_call(
        condense_body, [(4 * s, g.shape[1]), big], g, coupling[0], sep_block[0], iface_rows[0], pole,
        smem=1, us=3.0, loose=(3,), hbm=(0, 1, 2),
        scratch=[pltpu.VMEM(a, F32) for a in (g.shape, coupling.shape[1:], (s, s))] + [pltpu.SemaphoreType.DMA((4,))],
    )
    outs = [big, square, square, big]
    k, part, w, inv, far = kernel_call(
        core_join_body, [big] + outs[1:2] + outs[1:], k, flip(k, 1), core, smem=1, us=3.5
    )
    joins = [(w, inv, far)]
    one = flip(part, 2)
    k, w, inv, far = kernel_call(side_join_body, outs, k, one, flip(one, 1), core, flags[1:2], smem=2, us=3.5)
    joins.append((w, inv, far))
    for level in range(2, 4):
        his = flip(k, 1 << level)
        k, w, inv, far = kernel_call(join_body, outs, k, his, flags[level : level + 1], smem=1, us=3.5)
        joins.append((w, inv, far))
    k_end, inv_end, back, fore = kernel_call(end_body, [(s, 2 * s)] + [square] * 3, k, flags[4:], smem=1, us=3.5)
    (inv_mid,) = kernel_call(middle_body, [square], k_end, flip(k_end, 16), us=3.5)

    (base,) = kernel_call(base_body, [(g.shape[1], cols)], g, y, pole, smem=1, us=2.0, loose_outs=True)
    r, sent = kernel_call(rights_body, [(4 * s, half)] * 2, vt, y, y_separator[0], core, smem=1, us=0.7, loose=(2,))
    solved = []
    for level, (w, inv, far) in enumerate(joins):
        his = flip(sent if level == 0 else r, 1 << level)
        r, v = kernel_call(
            sides_body, [(4 * s, half), (2 * s, half)], r, his, inv, far, flags[level : level + 1],
            smem=1, us=0.5,
        )
        solved += [w, v]
    r_end, v_end = kernel_call(end_sides_body, [(2 * s, half)] * 2, r, inv_end, back, flags[4:], smem=1, us=0.4)
    own, sent = kernel_call(
        back_body, [(4 * s, half)] * 2, inv_mid, r_end, flip(r_end, 16), fore, v_end, *solved, flags,
        smem=1, us=1.5,
    )
    (total,) = kernel_call(
        field_body, [(4, 4, 2 * rows + s // 8, half)], base, vt, own, flip(sent, 1), pole, core,
        smem=2, loose=(0,),
    )
    total = exchange(total, groups_x).sum(0)
    total = exchange(total, groups_z)
    field, sep = kernel_call(close_body, [(rows, cols), (s // 16, cols)], total, us=0.2, loose_outs=True)
    return field[None], sep[None]


def solution(mesh):
    return jax.shard_map(
        shards,
        mesh=mesh,
        in_specs=(
            P("dom", "pole", None),
            P("dom", None, None),
            P(None, "pole", "dom", None, None),
            P(None, "pole"),
            P("dom", None, None, None),
            P("dom", None, None),
            P("dom", None, None),
        ),
        out_specs=(P("dom", "pole", None), P("dom", "pole", None)),
        check_vma=False,
    )
```

time: 210 us -> 135 us (0.64)
  waiting for transfers between devices: 41.7 us -> 6.21 us
  local copies, waits for them, and re-layouts: 22.3 us -> 3.71 us
  starting transfers between devices: 48.5 us -> 62.6 us
  Pallas kernels: 47.8 us -> 35.2 us
  blocking collectives: 37.3 us -> 25.6 us
  other arithmetic: 10 us -> 0.03 us
    ppermute x13 -> x12, waiting for transfers between devices: 38.4 us -> 6.2 us  [flip(): return lax.ppermute(x, 'dom', [(i, i ^ k) for i in range(doms)])]
    pallas_call x11 -> x17, Pallas kernels: 47.8 us -> 35.2 us  [kernel_call(): pl.pallas_call(body, out_shape=[jax.ShapeDtypeStruct(o, F32) if loose_out...]
    slice x26 -> x0, local copies, waits for them, and re-layouts: 12 us -> none  [the longest x3 1.9 us: shards(): down[:, 2 * s:]]
    all_to_all x3 -> x2, blocking collectives: 37.3 us -> 25.6 us  [exchange(): return lax.all_to_all(a, 'pole', 0, 0, tiled=True, axis_index_groups=groups)]
    select_n x9 -> x0, other arithmetic: 8.45 us -> none  [the longest x1 1.73 us: shards(): mine = jnp.where(side == 0, r1[:, :quarter], r1[:, quarter:])]
    all_to_all x1 -> x2, starting transfers between devices: 4.29 us -> 11.5 us  [exchange(): return lax.all_to_all(a, 'pole', 0, 0, tiled=True, axis_index_groups=groups)]
    ppermute x13 -> x12, starting transfers between devices: 44.2 us -> 51.1 us  [flip(): return lax.ppermute(x, 'dom', [(i, i ^ k) for i in range(doms)])]
    all_to_all x1 -> x2, waiting for transfers between devices: 3.34 us -> 0.01 us  [exchange(): return lax.all_to_all(a, 'pole', 0, 0, tiled=True, axis_index_groups=groups)]
  transfers between devices with their start and end apart: 14 -> 14, of which waited for: 14 -> 3; matrix products, arithmetic and copies ran while one was open for 2% -> 1% of each run, Pallas kernels for 2% -> 23%
where the time goes in v2:
time: 135 us; the launch traced here: 134 us
  starting transfers between devices  62.6 us (46%)
  Pallas kernels  35.2 us (26%)
  blocking collectives  25.6 us (19%)
  waiting for transfers between devices  6.21 us (5%)
  local copies, waits for them, and re-layouts  3.71 us (3%)
    ppermute x12, starting transfers between devices, flip(): return lax.ppermute(x, 'dom', [(i, i ^ k) for i in range(doms)])  51.1 us
    pallas_call x17, Pallas kernels, kernel_call(): pl.pallas_call(body, out_shape=[jax.ShapeDtypeStruct(o, F32) if loose_out...  35.2 us
    all_to_all x2, blocking collectives, exchange(): return lax.all_to_all(a, 'pole', 0, 0, tiled=True, axis_index_groups=groups)  25.6 us
    all_to_all x2, starting transfers between devices, exchange(): return lax.all_to_all(a, 'pole', 0, 0, tiled=True, axis_index_groups=groups)  11.5 us
    ppermute x12, waiting for transfers between devices, flip(): return lax.ppermute(x, 'dom', [(i, i ^ k) for i in range(doms)])  6.2 us
  transfers between devices with their start and end apart: 14, of which 3 were waited for; matrix products, arithmetic and copies ran while one was open for 1% of the time, Pallas kernels for 23%

profile of v2, /device:TPU:8, one launch (start us, length us, event | category | flops | bytes accessed | tf_op | source)
XLA Modules:
  0.0 134.4 jit_solution(3843770408600728960)
XLA Ops:
  0.6 1.4 %broadcast_in_dim.20 = f32[4,32,256]{2,1,0:T(8,128)} broadcast(f32[32,256]{1,0:T(8,128)} %bitcast.21), dimensions={1,2} | broadcast | bytes 163840 | tf_op jit(solution)/shard_map/broadcast_in_dim | solution.py:324
  2.0 7.3 %all-to-all-start = ((f32[4,32,256]{2,1,0:T(8,128)}), f32[4,32,256]{2,1,0:T(8,128)S(1)}, u32[]{:S(2)}, u32[]{:S(2)}) async-start(f32[4,32,256]{2,1,0:T(8,128)} %broadcast_in_dim.20), calls=%async_computation | async-start | bytes 262144 | tf_op jit(solution)/shard_map/all_to_all | solution.py:322
  9.3 0.7 copy-done.2
  10.6 4.4 %shard_map.87 = (f32[256,512]{1,0:T(8,128)S(1)}, f32[256,128]{1,0:T(8,128)S(1)}) custom-call(f32[2,512,512]{2,1,0:T(8,128)} %bitcast.14, f32[2,64,128]{2,1,0:T(8,128)} %bitcast.22, f32[64,64]{1,0:T(8,128)} %bitcast.23, s32[2,128]{1,0:T(2,128)S(1)} %bitcast.17, f32[4]{0:T(128)S(1)} %bitcast.18), custom_call_target="tpu_custom_call" | custom-call | flops 3000000000 | bytes 65536 | tf_op jit(solution)/shard_map/pallas_call | solution.py:105
  15.1 1.9 %collective-permute-start = (f32[256,128]{1,0:T(8,128)S(1)}, f32[256,128]{1,0:T(8,128)S(1)}, u32[]{:S(2)}, u32[]{:S(2)}) collective-permute-start(f32[256,128]{1,0:T(8,128)S(1)} %get-tuple-element.42.mine_ref), channel_id=1, source_target_pairs={{0,1},{1,0},{2,3},{3,2},{4,5},{5,4},{6,7},{7,6},{8,9},{9,8},{10,11... | collective-permute-start | bytes 393224 | tf_op jit(solution)/shard_map/ppermute | solution.py:319
  17.0 0.9 broadcast_in_dim.21
  17.9 4.3 %all-to-all-start.1 = ((f32[4,4,32,256]{3,2,1,0:T(8,128)}), f32[4,4,32,256]{3,2,1,0:T(8,128)S(1)}, u32[]{:S(2)}, u32[]{:S(2)}) async-start(f32[4,4,32,256]{3,2,1,0:T(8,128)} %broadcast_in_dim.21), calls=%async_computation.1 | async-start | bytes 1048576 | tf_op jit(solution)/shard_map/all_to_all | solution.py:322
  22.2 3.6 %shard_map.88 = (f32[256,128]{1,0:T(8,128)S(1)}, f32[128,128]{1,0:T(8,128)S(1)}, f32[128,128]{1,0:T(8,128)S(1)}, f32[128,128]{1,0:T(8,128)S(1)}, f32[256,128]{1,0:T(8,128)S(1)}) custom-call(f32[256,128]{1,0:T(8,128)S(1)} %get-tuple-element.42.mine_ref, f32[256,128]{1,0:T(8,128)S(1)} %collective-permute-done.his_ref, s32[1]{0:T(128)} %bitcast.6.core_ref.flag_ref), custom_call_target="tpu_custom_call" | custom-call | flops 3500000000 | bytes 65536 | tf_op jit(solution)/shard_map/pallas_call | solution.py:105
  25.7 8.2 %collective-permute-start.1 = (f32[128,128]{1,0:T(8,128)S(1)}, f32[128,128]{1,0:T(8,128)S(1)}, u32[]{:S(2)}, u32[]{:S(2)}) collective-permute-start(f32[128,128]{1,0:T(8,128)S(1)} %get-tuple-element.44), channel_id=1, source_target_pairs={{0,2},{1,3},{2,0},{3,1},{4,6},{5,7},{6,4},{7,5},{8,10},{9,11},{10,... | collective-permute-start | bytes 196616 | tf_op jit(solution)/shard_map/ppermute | solution.py:319
  33.9 2.5 %collective-permute-done.1.one_ref = f32[128,128]{1,0:T(8,128)S(1)} collective-permute-done((f32[128,128]{1,0:T(8,128)S(1)}, f32[128,128]{1,0:T(8,128)S(1)}, u32[]{:S(2)}, u32[]{:S(2)}) %collective-permute-start.1) | collective-permute-done | bytes 65568 | tf_op jit(solution)/shard_map/ppermute | solution.py:319
  36.5 1.9 %collective-permute-start.2 = (f32[128,128]{1,0:T(8,128)S(1)}, f32[128,128]{1,0:T(8,128)S(1)}, u32[]{:S(2)}, u32[]{:S(2)}) collective-permute-start(f32[128,128]{1,0:T(8,128)S(1)} %collective-permute-done.1.one_ref), channel_id=1, source_target_pairs={{0,1},{1,0},{2,3},{3,2},{4,5},{5,4},{6,7},{7,6},{8,9},{9,8},{10,11... | collective-permute-start | bytes 196616 | tf_op jit(solution)/shard_map/ppermute | solution.py:319
  39.1 2.4 %collective-permute-start.6 = (f32[256,128]{1,0:T(8,128)S(1)}, f32[256,128]{1,0:T(8,128)S(1)}, u32[]{:S(2)}, u32[]{:S(2)}) collective-permute-start(f32[256,128]{1,0:T(8,128)S(1)} %get-tuple-element.50), channel_id=1, source_target_pairs={{0,1},{1,0},{2,3},{3,2},{4,5},{5,4},{6,7},{7,6},{8,9},{9,8},{10,11... | collective-permute-start | bytes 393224 | tf_op jit(solution)/shard_map/ppermute | solution.py:319
  41.5 3.6 %shard_map.89 = (f32[256,128]{1,0:T(8,128)S(1)}, f32[128,128]{1,0:T(8,128)S(1)}, f32[128,128]{1,0:T(8,128)S(1)}, f32[256,128]{1,0:T(8,128)S(1)}) custom-call(f32[256,128]{1,0:T(8,128)S(1)} %get-tuple-element.43.mine_ref, f32[128,128]{1,0:T(8,128)S(1)} %collective-permute-done.1.one_ref, f32[128,128]{1,0:T(8,128)S(1)} %collective-permute-done.2.two_ref, ...), custom_call_target="tpu_custom_call" | custom-call | flops 3500000000 | bytes 65536 | tf_op jit(solution)/shard_map/pallas_call | solution.py:105
  45.1 2.6 %collective-permute-start.3 = (f32[256,128]{1,0:T(8,128)S(1)}, f32[256,128]{1,0:T(8,128)S(1)}, u32[]{:S(2)}, u32[]{:S(2)}) collective-permute-start(f32[256,128]{1,0:T(8,128)S(1)} %get-tuple-element.45.mine_ref), channel_id=1, source_target_pairs={{0,4},{1,5},{2,6},{3,7},{4,0},{5,1},{6,2},{7,3},{8,12},{9,13},{10,... | collective-permute-start | bytes 393224 | tf_op jit(solution)/shard_map/ppermute | solution.py:319
  48.2 8.4 %collective-permute-start.7 = (f32[256,128]{1,0:T(8,128)S(1)}, f32[256,128]{1,0:T(8,128)S(1)}, u32[]{:S(2)}, u32[]{:S(2)}) collective-permute-start(f32[256,128]{1,0:T(8,128)S(1)} %get-tuple-element.53.mine_ref), channel_id=1, source_target_pairs={{0,2},{1,3},{2,0},{3,1},{4,6},{5,7},{6,4},{7,5},{8,10},{9,11},{10,... | collective-permute-start | bytes 393224 | tf_op jit(solution)/shard_map/ppermute | solution.py:319
  56.7 3.6 %shard_map.90 = (f32[256,128]{1,0:T(8,128)S(1)}, f32[128,128]{1,0:T(8,128)S(1)}, f32[128,128]{1,0:T(8,128)S(1)}, f32[256,128]{1,0:T(8,128)S(1)}) custom-call(f32[256,128]{1,0:T(8,128)S(1)} %get-tuple-element.45.mine_ref, f32[256,128]{1,0:T(8,128)S(1)} %collective-permute-done.3.his_ref, s32[1]{0:T(128)} %bitcast.8.flag_ref), custom_call_target="tpu_custom_call" | custom-call | flops 3500000000 | bytes 65536 | tf_op jit(solution)/shard_map/pallas_call | solution.py:105
  60.2 4.9 %collective-permute-start.4 = (f32[256,128]{1,0:T(8,128)S(1)}, f32[256,128]{1,0:T(8,128)S(1)}, u32[]{:S(2)}, u32[]{:S(2)}) collective-permute-start(f32[256,128]{1,0:T(8,128)S(1)} %get-tuple-element.46.mine_ref), channel_id=1, source_target_pairs={{0,8},{1,9},{2,10},{3,11},{4,12},{5,13},{6,14},{7,15},{8,0},{9,1},... | collective-permute-start | bytes 393224 | tf_op jit(solution)/shard_map/ppermute | solution.py:319
  65.8 3.5 %collective-permute-start.8 = (f32[256,128]{1,0:T(8,128)S(1)}, f32[256,128]{1,0:T(8,128)S(1)}, u32[]{:S(2)}, u32[]{:S(2)}) collective-permute-start(f32[256,128]{1,0:T(8,128)S(1)} %get-tuple-element.56.mine_ref), channel_id=1, source_target_pairs={{0,4},{1,5},{2,6},{3,7},{4,0},{5,1},{6,2},{7,3},{8,12},{9,13},{10,... | collective-permute-start | bytes 393224 | tf_op jit(solution)/shard_map/ppermute | solution.py:319
  69.3 1.1 collective-permute-done.4.his_ref
  70.4 3.6 %shard_map.91 = (f32[256,128]{1,0:T(8,128)S(1)}, f32[128,128]{1,0:T(8,128)S(1)}, f32[128,128]{1,0:T(8,128)S(1)}, f32[256,128]{1,0:T(8,128)S(1)}) custom-call(f32[256,128]{1,0:T(8,128)S(1)} %get-tuple-element.46.mine_ref, f32[256,128]{1,0:T(8,128)S(1)} %collective-permute-done.4.his_ref, s32[1]{0:T(128)} %bitcast.9.flag_ref), custom_call_target="tpu_custom_call" | custom-call | flops 3500000000 | bytes 65536 | tf_op jit(solution)/shard_map/pallas_call | solution.py:105
  74.5 5.3 %collective-permute-start.9 = (f32[256,128]{1,0:T(8,128)S(1)}, f32[256,128]{1,0:T(8,128)S(1)}, u32[]{:S(2)}, u32[]{:S(2)}) collective-permute-start(f32[256,128]{1,0:T(8,128)S(1)} %get-tuple-element.59.mine_ref), channel_id=1, source_target_pairs={{0,8},{1,9},{2,10},{3,11},{4,12},{5,13},{6,14},{7,15},{8,0},{9,1},... | collective-permute-start | bytes 393224 | tf_op jit(solution)/shard_map/ppermute | solution.py:319
  79.8 3.4 %shard_map.92 = (f32[64,128]{1,0:T(8,128)S(1)}, f32[128,128]{1,0:T(8,128)S(1)}, f32[128,128]{1,0:T(8,128)S(1)}, f32[128,128]{1,0:T(8,128)S(1)}) custom-call(f32[256,128]{1,0:T(8,128)S(1)} %get-tuple-element.47.k_ref, s32[1]{0:T(128)} %bitcast.10.flag_ref), custom_call_target="tpu_custom_call" | custom-call | flops 3500000000 | bytes 65536 | tf_op jit(solution)/shard_map/pallas_call | solution.py:105
  83.3 5.9 %collective-permute-start.5 = (f32[64,128]{1,0:T(8,128)S(1)}, f32[64,128]{1,0:T(8,128)S(1)}, u32[]{:S(2)}, u32[]{:S(2)}) collective-permute-start(f32[64,128]{1,0:T(8,128)S(1)} %get-tuple-element.48.mine_ref), channel_id=1, source_target_pairs={{0,16},{1,17},{2,18},{3,19},{4,20},{5,21},{6,22},{7,23},{8,24},{9,... | collective-permute-start | bytes 98312 | tf_op jit(solution)/shard_map/ppermute | solution.py:319
  90.3 4.0 %collective-permute-start.10 = (f32[128,128]{1,0:T(8,128)S(1)}, f32[128,128]{1,0:T(8,128)S(1)}, u32[]{:S(2)}, u32[]{:S(2)}) collective-permute-start(f32[128,128]{1,0:T(8,128)S(1)} %get-tuple-element.65.refs_1_), channel_id=1, source_target_pairs={{0,16},{1,17},{2,18},{3,19},{4,20},{5,21},{6,22},{7,23},{8,24},{9,... | collective-permute-start | bytes 196616 | tf_op jit(solution)/shard_map/ppermute | solution.py:319
  94.3 3.6 %shard_map.93.refs_0_ = f32[128,128]{1,0:T(8,128)S(1)} custom-call(f32[64,128]{1,0:T(8,128)S(1)} %get-tuple-element.48.mine_ref, f32[64,128]{1,0:T(8,128)S(1)} %collective-permute-done.5.his_ref), custom_call_target="tpu_custom_call" | custom-call | flops 3500000000 | bytes 65536 | tf_op jit(solution)/shard_map/pallas_call | solution.py:105
  97.9 2.6 %collective-permute-done.10.refs_2_ = f32[128,128]{1,0:T(8,128)S(1)} collective-permute-done((f32[128,128]{1,0:T(8,128)S(1)}, f32[128,128]{1,0:T(8,128)S(1)}, u32[]{:S(2)}, u32[]{:S(2)}) %collective-permute-start.10) | collective-permute-done | bytes 65568 | tf_op jit(solution)/shard_map/ppermute | solution.py:319
  100.5 2.0 %shard_map.100 = (f32[256,128]{1,0:T(8,128)S(1)}, f32[256,128]{1,0:T(8,128)S(1)}) custom-call(f32[128,128]{1,0:T(8,128)S(1)} %shard_map.93.refs_0_, f32[128,128]{1,0:T(8,128)S(1)} %get-tuple-element.65.refs_1_, f32[128,128]{1,0:T(8,128)S(1)} %collective-permute-done.10.refs_2_, f32[128,128]{1,0:T(8,128)S(1)} %get-tuple-element.66.refs_3_, ...), custom_call_target="tpu_custom_call" | custom-call | flops 1500000000 | bytes 65536 | tf_op jit(solution)/shard_map/pallas_call | solution.py:105
  102.5 1.9 %collective-permute-start.11 = (f32[256,128]{1,0:T(8,128)S(1)}, f32[256,128]{1,0:T(8,128)S(1)}, u32[]{:S(2)}, u32[]{:S(2)}) collective-permute-start(f32[256,128]{1,0:T(8,128)S(1)} %get-tuple-element.77), channel_id=1, source_target_pairs={{0,1},{1,0},{2,3},{3,2},{4,5},{5,4},{6,7},{7,6},{8,9},{9,8},{10,11... | collective-permute-start | bytes 393224 | tf_op jit(solution)/shard_map/ppermute | solution.py:319
  104.4 2.5 %shard_map.86.base_ref = f32[512,256]{1,0:T(8,128)S(1)} custom-call(f32[2,512,512]{2,1,0:T(8,128)S(1)} %bitcast.15, f32[4,4,32,256]{3,2,1,0:T(8,128)S(1)} %all-to-all-done.1.y_ref, f32[4]{0:T(128)S(1)} %bitcast.19), custom_call_target="tpu_custom_call" | custom-call | flops 2000000000 | bytes 65536 | tf_op jit(solution)/shard_map/pallas_call | solution.py:105
  107.0 1.2 shard_map.101
  108.1 15.4 %all_to_all.20 = f32[4,4,72,128]{3,2,1,0:T(8,128)S(1)} all-to-all(f32[4,4,72,128]{3,2,1,0:T(8,128)S(1)} %shard_map.101), channel_id=1, replica_groups={{0,32,64,96},{128,160,192,224},{256,288,320,352},{384,416,448,480},{1,3..., dimensions={0} | all-to-all | bytes 1179648 | tf_op jit(solution)/shard_map/all_to_all | solution.py:322
  123.5 10.2 %all_to_all.21.a_ref = f32[4,72,128]{2,1,0:T(8,128)S(1)} all-to-all(f32[4,72,128]{2,1,0:T(8,128)S(1)} %reduce_sum.9), channel_id=1, replica_groups={{0,128,256,384},{32,160,288,416},{64,192,320,448},{96,224,352,480},{1,1..., dimensions={0} | all-to-all | bytes 294912 | tf_op jit(solution)/shard_map/all_to_all | solution.py:322
  (29 shorter events, 4.7 us)
Async XLA Ops:
  2.0 14.9 %all-to-all-start = ((f32[4,32,256]{2,1,0:T(8,128)}), f32[4,32,256]{2,1,0:T(8,128)S(1)}, u32[]{:S(2)}, u32[]{:S(2)}) async-start(f32[4,32,256]{2,1,0:T(8,128)} %broadcast_in_dim.20), calls=%async_computation | async-start | bytes 262144 | tf_op jit(solution)/shard_map/all_to_all | solution.py:322
  9.3 0.7 copy-start.2
  10.0 0.7 copy-start.3
  15.1 7.1 %collective-permute-start = (f32[256,128]{1,0:T(8,128)S(1)}, f32[256,128]{1,0:T(8,128)S(1)}, u32[]{:S(2)}, u32[]{:S(2)}) collective-permute-start(f32[256,128]{1,0:T(8,128)S(1)} %get-tuple-element.42.mine_ref), channel_id=1, source_target_pairs={{0,1},{1,0},{2,3},{3,2},{4,5},{5,4},{6,7},{7,6},{8,9},{9,8},{10,11... | collective-permute-start | bytes 393224 | tf_op jit(solution)/shard_map/ppermute | solution.py:319
  17.9 20.5 %all-to-all-start.1 = ((f32[4,4,32,256]{3,2,1,0:T(8,128)}), f32[4,4,32,256]{3,2,1,0:T(8,128)S(1)}, u32[]{:S(2)}, u32[]{:S(2)}) async-start(f32[4,4,32,256]{3,2,1,0:T(8,128)} %broadcast_in_dim.21), calls=%async_computation.1 | async-start | bytes 1048576 | tf_op jit(solution)/shard_map/all_to_all | solution.py:322
  22.2 16.3 %copy-start.1 = (f32[1,64,256]{2,1,0:T(8,128)S(1)}, f32[1,64,256]{2,1,0:T(8,128)}, u32[]{:S(2)}) copy-start(f32[1,64,256]{2,1,0:T(8,128)} %param.8) | copy-start | bytes 196612
  25.7 10.8 %collective-permute-start.1 = (f32[128,128]{1,0:T(8,128)S(1)}, f32[128,128]{1,0:T(8,128)S(1)}, u32[]{:S(2)}, u32[]{:S(2)}) collective-permute-start(f32[128,128]{1,0:T(8,128)S(1)} %get-tuple-element.44), channel_id=1, source_target_pairs={{0,2},{1,3},{2,0},{3,1},{4,6},{5,7},{6,4},{7,5},{8,10},{9,11},{10,... | collective-permute-start | bytes 196616 | tf_op jit(solution)/shard_map/ppermute | solution.py:319
  36.5 5.0 %collective-permute-start.2 = (f32[128,128]{1,0:T(8,128)S(1)}, f32[128,128]{1,0:T(8,128)S(1)}, u32[]{:S(2)}, u32[]{:S(2)}) collective-permute-start(f32[128,128]{1,0:T(8,128)S(1)} %collective-permute-done.1.one_ref), channel_id=1, source_target_pairs={{0,1},{1,0},{2,3},{3,2},{4,5},{5,4},{6,7},{7,6},{8,9},{9,8},{10,11... | collective-permute-start | bytes 196616 | tf_op jit(solution)/shard_map/ppermute | solution.py:319
  39.1 8.6 %collective-permute-start.6 = (f32[256,128]{1,0:T(8,128)S(1)}, f32[256,128]{1,0:T(8,128)S(1)}, u32[]{:S(2)}, u32[]{:S(2)}) collective-permute-start(f32[256,128]{1,0:T(8,128)S(1)} %get-tuple-element.50), channel_id=1, source_target_pairs={{0,1},{1,0},{2,3},{3,2},{4,5},{5,4},{6,7},{7,6},{8,9},{9,8},{10,11... | collective-permute-start | bytes 393224 | tf_op jit(solution)/shard_map/ppermute | solution.py:319
  45.1 11.6 %collective-permute-start.3 = (f32[256,128]{1,0:T(8,128)S(1)}, f32[256,128]{1,0:T(8,128)S(1)}, u32[]{:S(2)}, u32[]{:S(2)}) collective-permute-start(f32[256,128]{1,0:T(8,128)S(1)} %get-tuple-element.45.mine_ref), channel_id=1, source_target_pairs={{0,4},{1,5},{2,6},{3,7},{4,0},{5,1},{6,2},{7,3},{8,12},{9,13},{10,... | collective-permute-start | bytes 393224 | tf_op jit(solution)/shard_map/ppermute | solution.py:319
  48.2 17.0 %collective-permute-start.7 = (f32[256,128]{1,0:T(8,128)S(1)}, f32[256,128]{1,0:T(8,128)S(1)}, u32[]{:S(2)}, u32[]{:S(2)}) collective-permute-start(f32[256,128]{1,0:T(8,128)S(1)} %get-tuple-element.53.mine_ref), channel_id=1, source_target_pairs={{0,2},{1,3},{2,0},{3,1},{4,6},{5,7},{6,4},{7,5},{8,10},{9,11},{10,... | collective-permute-start | bytes 393224 | tf_op jit(solution)/shard_map/ppermute | solution.py:319
  60.2 10.1 %collective-permute-start.4 = (f32[256,128]{1,0:T(8,128)S(1)}, f32[256,128]{1,0:T(8,128)S(1)}, u32[]{:S(2)}, u32[]{:S(2)}) collective-permute-start(f32[256,128]{1,0:T(8,128)S(1)} %get-tuple-element.46.mine_ref), channel_id=1, source_target_pairs={{0,8},{1,9},{2,10},{3,11},{4,12},{5,13},{6,14},{7,15},{8,0},{9,1},... | collective-permute-start | bytes 393224 | tf_op jit(solution)/shard_map/ppermute | solution.py:319
  65.8 8.1 %collective-permute-start.8 = (f32[256,128]{1,0:T(8,128)S(1)}, f32[256,128]{1,0:T(8,128)S(1)}, u32[]{:S(2)}, u32[]{:S(2)}) collective-permute-start(f32[256,128]{1,0:T(8,128)S(1)} %get-tuple-element.56.mine_ref), channel_id=1, source_target_pairs={{0,4},{1,5},{2,6},{3,7},{4,0},{5,1},{6,2},{7,3},{8,12},{9,13},{10,... | collective-permute-start | bytes 393224 | tf_op jit(solution)/shard_map/ppermute | solution.py:319
  74.5 14.8 %collective-permute-start.9 = (f32[256,128]{1,0:T(8,128)S(1)}, f32[256,128]{1,0:T(8,128)S(1)}, u32[]{:S(2)}, u32[]{:S(2)}) collective-permute-start(f32[256,128]{1,0:T(8,128)S(1)} %get-tuple-element.59.mine_ref), channel_id=1, source_target_pairs={{0,8},{1,9},{2,10},{3,11},{4,12},{5,13},{6,14},{7,15},{8,0},{9,1},... | collective-permute-start | bytes 393224 | tf_op jit(solution)/shard_map/ppermute | solution.py:319
  83.3 11.0 %collective-permute-start.5 = (f32[64,128]{1,0:T(8,128)S(1)}, f32[64,128]{1,0:T(8,128)S(1)}, u32[]{:S(2)}, u32[]{:S(2)}) collective-permute-start(f32[64,128]{1,0:T(8,128)S(1)} %get-tuple-element.48.mine_ref), channel_id=1, source_target_pairs={{0,16},{1,17},{2,18},{3,19},{4,20},{5,21},{6,22},{7,23},{8,24},{9,... | collective-permute-start | bytes 98312 | tf_op jit(solution)/shard_map/ppermute | solution.py:319
  90.3 10.2 %collective-permute-start.10 = (f32[128,128]{1,0:T(8,128)S(1)}, f32[128,128]{1,0:T(8,128)S(1)}, u32[]{:S(2)}, u32[]{:S(2)}) collective-permute-start(f32[128,128]{1,0:T(8,128)S(1)} %get-tuple-element.65.refs_1_), channel_id=1, source_target_pairs={{0,16},{1,17},{2,18},{3,19},{4,20},{5,21},{6,22},{7,23},{8,24},{9,... | collective-permute-start | bytes 196616 | tf_op jit(solution)/shard_map/ppermute | solution.py:319
  100.5 3.9 %copy-start = (f32[2,1,1,512,512]{4,3,2,1,0:T(8,128)S(1)}, f32[2,1,1,512,512]{4,3,2,1,0:T(8,128)}, u32[]{:S(2)}) copy-start(f32[2,1,1,512,512]{4,3,2,1,0:T(8,128)} %param.9) | copy-start | bytes 6291460
  100.5 3.9 %copy-start.4 = (f32[4,1]{0,1:T(1,128)S(1)}, f32[4,1]{0,1:T(1,128)}, u32[]{:S(2)}) copy-start(f32[4,1]{0,1:T(1,128)} %param.10) | copy-start | bytes 52
  102.5 4.5 %collective-permute-start.11 = (f32[256,128]{1,0:T(8,128)S(1)}, f32[256,128]{1,0:T(8,128)S(1)}, u32[]{:S(2)}, u32[]{:S(2)}) collective-permute-start(f32[256,128]{1,0:T(8,128)S(1)} %get-tuple-element.77), channel_id=1, source_target_pairs={{0,1},{1,0},{2,3},{3,2},{4,5},{5,4},{6,7},{7,6},{8,9},{9,8},{10,11... | collective-permute-start | bytes 393224 | tf_op jit(solution)/shard_map/ppermute | solution.py:319
